TPU v7x, 512 devices: a whole 4x8x8 slice. The times are simulated.
512 devices in a mesh: grp: 32 (over y_lo, z, core), blk: 16 (over x, y_hi).
Axes of the slice: x: 4, y: 8 (y_hi: 4, y_lo: 2; y = y_hi * 2 + y_lo), z: 8, core: 2. Of those that a mesh axis runs over, the one named last changes fastest.
Arguments:
- child_inverse: bfloat16 [32, 2, 2048, 2048], P('grp', None, 'blk'), may hold values from -0.09375 to 0.09375
- border_block: bfloat16 [32, 2, 2048, 2048], P('grp', None, 'blk'), may hold values from -0.09375 to 0.09375
- child_rhs: bfloat16 [32, 2, 2048, 256], P('grp', None, 'blk'), may hold values from -6 to 6
- parent_inverse: bfloat16 [32, 2, 4096, 2048], P('grp', None, 'blk'), may hold values from -0.0625 to 0.0625
- parent_rhs: bfloat16 [32, 2, 2048, 256], P('grp', None, 'blk'), may hold values from -6 to 6
- parent_of: int32 [32, 1], replicated, may hold values from 0 to 15
- owner: int32 [16], replicated, may hold values from 0 to 15, each once
- row_map: int32 [32, 2048], replicated, may hold values from 0 to 4095, as said below
Outputs:
- child_solution: bfloat16 [32, 2, 2048, 256], P('grp', None, 'blk')
- parent_solution: bfloat16 [32, 2, 2048, 256], P('grp', None, 'blk')
Inputs may be any that keep to these rules, and one draw needn't show every extreme that they name: parent_of[c, 0] is the parent front of the sibling front on group c; every parent front has one sibling or more. owner[p] names the pair of groups 2 owner[p] and 2 owner[p] + 1 that holds parent front p; each pair holds one parent. row_map[c, j] differ for different j of one c; border row j with j // 128 = b goes to a parent row h * 2048 + b * 128 + r with h of 0 or 1 and r < 128.
All inputs are finite; a program needn't handle non-finite values.
Results may differ from a plain program's by a relative error of at most 0.008.
Values may be sent and summed in bfloat16 or wider, within the bound.
No kernel may reach another device: no remote copies, remote signals or barrier semaphores. Data moves between devices by JAX's collectives and lax.ppermute only.
A program may use at most 64 MiB of HBM per device.

v0:
```python
import functools

import jax
import jax.numpy as jnp
from jax import lax
from jax.experimental import pallas as pl
from jax.experimental.pallas import tpu as pltpu
from jax.sharding import PartitionSpec as P


F32 = jnp.float32
BF16 = jnp.bfloat16
GROUPS = 32
SIDE = 4
LIMIT = 12 << 20
VM = pl.BlockSpec(memory_space=pltpu.VMEM)
SM = pl.BlockSpec(memory_space=pltpu.SMEM)


def cost(flops, moved):
    return pl.CostEstimate(flops=flops, bytes_accessed=moved, transcendentals=0)


def products(matrix, g_ref):
    rows, inner = matrix.shape[1:]
    cols = g_ref.shape[-1]
    both = matrix.reshape(2 * rows, inner)
    with_real = jnp.dot(both, g_ref[:, 0].reshape(inner, cols), preferred_element_type=F32)
    with_imag = jnp.dot(both, g_ref[:, 1].reshape(inner, cols), preferred_element_type=F32)
    return with_real[:rows] - with_imag[rows:], with_imag[:rows] + with_real[rows:]


def slice_kernel(x_ref, *refs):
    *m_refs, o_ref = refs
    for which, m_ref in enumerate(m_refs):
        o_ref[which] = m_ref[...]


def child_kernel(which, x_ref, *refs):
    *m_refs, g_ref, o_ref = refs
    for shift, m_ref in enumerate(m_refs):
        block = lax.rem(x_ref[0] + SIDE - shift, SIDE)
        for part, value in enumerate(products(m_ref[which], g_ref)):
            o_ref[block, part] = value.astype(BF16)


def parent_kernel(x_ref, *refs):
    *m_refs, g_ref, kept_ref, given_ref = refs
    rows = kept_ref.shape[2]
    half = x_ref[1]
    for shift, m_ref in enumerate(m_refs):
        block = lax.rem(x_ref[0] + SIDE - shift, SIDE)
        for part, value in enumerate(products(m_ref[0], g_ref)):
            top, low = value[:rows], value[rows:]
            kept_ref[block, part] = jnp.where(half == 0, top, low).astype(BF16)
            given_ref[block, part] = jnp.where(half == 0, low, top).astype(BF16)


def joined_kernel(a_ref, b_ref, o_ref):
    o_ref[...] = (a_ref[...].astype(F32) + b_ref[...].astype(F32)).astype(BF16)


def total(p_ref, part):
    value = p_ref[0, part].astype(F32)
    for block in range(1, p_ref.shape[0]):
        value += p_ref[block, part].astype(F32)
    return value


def pieces_kernel(p_ref, o_ref):
    wide = jnp.concatenate([-total(p_ref, part).T for part in range(2)], axis=0)
    o_ref[...] = wide.astype(BF16).reshape(o_ref.shape)


def total_kernel(p_ref, o_ref):
    for part in range(2):
        o_ref[part] = total(p_ref, part).astype(BF16)


def route_kernel(parent_ref, owner_ref, rows_ref, v_ref, o_ref, sums_ref):
    rows = v_ref.shape[2]
    sums_ref[...] = jnp.zeros_like(sums_ref)
    slots = lax.broadcasted_iota(jnp.int32, (2 * rows, rows), 0)
    for child in range(GROUPS):
        wanted = jnp.broadcast_to(rows_ref[child : child + 1, :], (2 * rows, rows))
        table = jnp.where(slots == wanted, 1.0, 0.0).astype(BF16)
        placed = lax.dot_general(
            v_ref[child], table, (((1,), (1,)), ((), ())), preferred_element_type=F32
        )
        pair = owner_ref[parent_ref[child]]
        sums_ref[pair] += placed
    for pair in range(GROUPS // 2):
        for half in range(2):
            o_ref[2 * pair + half] = sums_ref[pair, :, half * rows : (half + 1) * rows].astype(BF16)


def right_kernel(b_ref, p_ref, o_ref):
    cols = p_ref.shape[2]
    flat = b_ref[...].reshape(2 * cols, b_ref.shape[2]).astype(F32)
    for part in range(2):
        value = p_ref[part].astype(F32) + flat[part * cols : (part + 1) * cols].T
        o_ref[part] = value.astype(BF16)


def local(kernel, outs, flops, *operands, scalars=0):
    moved = sum(x.size * x.dtype.itemsize for x in operands)
    shapes = [jax.ShapeDtypeStruct(shape, BF16) for shape in outs]
    return pl.pallas_call(
        kernel,
        out_shape=shapes if len(shapes) > 1 else shapes[0],
        in_specs=[SM] * scalars + [VM] * (len(operands) - scalars),
        out_specs=[VM] * len(shapes) if len(shapes) > 1 else VM,
        cost_estimate=cost(flops, moved + 2 * sum(x.size for x in shapes)),
        compiler_params=pltpu.CompilerParams(vmem_limit_bytes=LIMIT),
    )(*operands)


def column_slice(here, shift, *matrices):
    rows, inner = matrices[0].shape[1:]
    shape = (2, rows, inner // SIDE)
    out = (len(matrices),) + shape
    return pl.pallas_call(
        slice_kernel,
        out_shape=jax.ShapeDtypeStruct(out, BF16),
        grid_spec=pltpu.PrefetchScalarGridSpec(
            num_scalar_prefetch=1,
            grid=(1,),
            in_specs=[
                pl.BlockSpec(shape, lambda i, x: (0, 0, lax.rem(x[0] + shift, SIDE)))
                for _ in matrices
            ],
            out_specs=pl.BlockSpec(out, lambda i, x: (0, 0, 0, 0)),
        ),
        cost_estimate=cost(0, 4 * len(matrices) * shape[0] * shape[1] * shape[2]),
        compiler_params=pltpu.CompilerParams(vmem_limit_bytes=LIMIT),
    )(here, *matrices)


def redistributed(here, *matrices):
    moved = [shifted(column_slice(here, k, *matrices), k) for k in range(1, SIDE)]
    return [column_slice(here, 0, *matrices)] + moved


def route(parent_of, owner, rows_of, pieces):
    width, rows = pieces.shape[1:]
    return pl.pallas_call(
        route_kernel,
        out_shape=jax.ShapeDtypeStruct(pieces.shape, BF16),
        in_specs=[SM, SM, VM, VM],
        out_specs=VM,
        scratch_shapes=[pltpu.VMEM((GROUPS // 2, width, 2 * rows), F32)],
        cost_estimate=cost(4 * GROUPS * width * rows * rows, 4 * GROUPS * width * rows),
        compiler_params=pltpu.CompilerParams(vmem_limit_bytes=LIMIT),
    )(parent_of, owner, rows_of, pieces)


ALONG_Y = [[i * SIDE + j for j in range(SIDE)] for i in range(SIDE)]
ALONG_X = [[i * SIDE + j for i in range(SIDE)] for j in range(SIDE)]


def over(blocks, axis, groups=None):
    return lax.all_to_all(blocks, axis, 0, 0, axis_index_groups=groups, tiled=True)


def shifted(block, shift):
    pairs = [
        (i * SIDE + j, (i + shift) % SIDE * SIDE + j) for i in range(SIDE) for j in range(SIDE)
    ]
    return lax.ppermute(block, "blk", pairs)


def along_y(block):
    return lax.all_gather(block, "blk", axis=0, tiled=False, axis_index_groups=ALONG_Y)


def along_x(blocks):
    return over(blocks, "blk", ALONG_X)


def per_device(
    child_inverse, border_block, child_rhs, parent_inverse, parent_rhs, parent_of, owner, row_map
):
    slot_index = lax.axis_index("blk")
    group_index = lax.axis_index("grp")
    rows, cols = child_rhs.shape[2:]
    block = (2, rows, cols)
    fan = (SIDE,) + block
    flops = 8 * rows * cols * child_inverse.shape[3]
    local_map = lax.dynamic_slice_in_dim(row_map, slot_index * rows, rows, 1)
    half_order = SIDE * SIDE * rows
    rows_of = (local_map // half_order) * rows + local_map % rows
    here = jnp.stack([slot_index // SIDE, group_index % 2]).astype(jnp.int32)

    child = redistributed(here, child_inverse[0], border_block[0])
    source = along_y(child_rhs[0])
    parts = local(functools.partial(child_kernel, 0), [fan], flops, here, *child, source, scalars=1)
    parts = along_x(parts)
    solved = local(total_kernel, [block], 0, parts)
    source = along_y(solved)
    parts = local(functools.partial(child_kernel, 1), [fan], flops, here, *child, source, scalars=1)
    parts = along_x(parts)
    pieces = local(pieces_kernel, [(GROUPS, 2 * cols // GROUPS, rows)], 0, parts)
    parent = redistributed(here, parent_inverse[0])
    columns = over(pieces, "grp")
    sums = route(parent_of[:, 0], owner, rows_of, columns)
    sums = over(sums, "grp")
    right = local(right_kernel, [block], 0, sums, parent_rhs[0])
    source = along_y(right)
    kept, given = local(parent_kernel, [fan, fan], 2 * flops, here, *parent, source, scalars=1)
    taken = lax.ppermute(given, "grp", [(i, i ^ 1) for i in range(GROUPS)])
    parts = local(joined_kernel, [fan], 0, kept, taken)
    parts = along_x(parts)
    answer = local(total_kernel, [block], 0, parts)
    return solved[None], answer[None]


def solution(mesh):
    spec = P("grp", None, "blk", None)
    return jax.shard_map(
        per_device,
        mesh=mesh,
        in_specs=(spec,) * 5 + (P(), P(), P()),
        out_specs=(spec, spec),
        check_vma=False,
    )
```

profile of v0, /device:TPU:1, one launch (start us, length us, event | category | flops | bytes accessed | tf_op | source)
XLA Modules:
  0.0 162.0 jit_solution(6536725254451553485)
XLA Ops:
  0.7 1.2 copy-done.1
  2.0 1.2 copy-done.2
  3.8 3.9 %collective-permute-start = (bf16[2,2,128,512]{3,2,1,0:T(8,128)(2,1)S(1)}, bf16[2,2,128,512]{3,2,1,0:T(8,128)(2,1)S(1)}, u32[]{:S(2)}, u32[]{:S(2)}) collective-permute-start(bf16[2,2,128,512]{3,2,1,0:T(8,128)(2,1)S(1)} %shard_map.96), channel_id=1, source_target_pairs={{0,4},{1,5},{2,6},{3,7},{4,8},{5,9},{6,10},{7,11},{8,12},{9,13},{1... | collective-permute-start | bytes 1572872 | tf_op jit(solution)/shard_map/ppermute | solution.py:169
  7.7 0.6 shard_map.97
  8.3 4.5 %collective-permute-start.1 = (bf16[2,2,128,512]{3,2,1,0:T(8,128)(2,1)S(1)}, bf16[2,2,128,512]{3,2,1,0:T(8,128)(2,1)S(1)}, u32[]{:S(2)}, u32[]{:S(2)}) collective-permute-start(bf16[2,2,128,512]{3,2,1,0:T(8,128)(2,1)S(1)} %shard_map.97), channel_id=1, source_target_pairs={{0,8},{1,9},{2,10},{3,11},{4,12},{5,13},{6,14},{7,15},{8,0},{9,1},... | collective-permute-start | bytes 1572872 | tf_op jit(solution)/shard_map/ppermute | solution.py:169
  13.4 3.1 %collective-permute-start.2 = (bf16[2,2,128,512]{3,2,1,0:T(8,128)(2,1)S(1)}, bf16[2,2,128,512]{3,2,1,0:T(8,128)(2,1)S(1)}, u32[]{:S(2)}, u32[]{:S(2)}) collective-permute-start(bf16[2,2,128,512]{3,2,1,0:T(8,128)(2,1)S(1)} %shard_map.98), channel_id=1, source_target_pairs={{0,12},{1,13},{2,14},{3,15},{4,0},{5,1},{6,2},{7,3},{8,4},{9,5},{1... | collective-permute-start | bytes 1572872 | tf_op jit(solution)/shard_map/ppermute | solution.py:169
  17.1 15.8 %all_gather.13.refs_4_ = bf16[4,2,128,256]{3,2,1,0:T(8,128)(2,1)S(1)} all-gather(bf16[1,2,128,256]{3,2,1,0:T(8,128)(2,1)S(1)} %copy-done.8), channel_id=1, replica_groups={{0,1,2,3},{4,5,6,7},{8,9,10,11},{12,13,14,15},{16,17,18,19},{20,21,22,2..., dimensions={0}, use_global_device_ids=true | all-gather | bytes 655360 | tf_op jit(solution)/shard_map/all_gather | solution.py:173
  32.9 1.3 shard_map.99
  34.1 12.4 %all_to_all.25.p_ref = bf16[4,2,128,256]{3,2,1,0:T(8,128)(2,1)S(1)} all-to-all(bf16[4,2,128,256]{3,2,1,0:T(8,128)(2,1)S(1)} %shard_map.99), channel_id=1, replica_groups={{0,4,8,12},{1,5,9,13},{2,6,10,14},{3,7,11,15},{16,20,24,28},{17,21,25,2..., dimensions={0} | all-to-all | bytes 1048576 | tf_op jit(solution)/shard_map/all_to_all | solution.py:162
  46.5 0.7 shard_map.100
  47.2 19.8 %all-gather = bf16[8,128,256]{2,1,0:T(8,128)(2,1)S(1)} all-gather(bf16[2,128,256]{2,1,0:T(8,128)(2,1)} %shard_map.100), channel_id=2, replica_groups={{0,1,2,3},{4,5,6,7},{8,9,10,11},{12,13,14,15},{16,17,18,19},{20,21,22,2..., dimensions={0}, use_global_device_ids=true | all-gather | bytes 655360 | tf_op jit(solution)/shard_map/all_gather | solution.py:173
  67.0 1.2 shard_map.105
  68.3 9.3 %all_to_all.26.p_ref = bf16[4,2,128,256]{3,2,1,0:T(8,128)(2,1)S(1)} all-to-all(bf16[4,2,128,256]{3,2,1,0:T(8,128)(2,1)S(1)} %shard_map.105), channel_id=1, replica_groups={{0,4,8,12},{1,5,9,13},{2,6,10,14},{3,7,11,15},{16,20,24,28},{17,21,25,2..., dimensions={0} | all-to-all | bytes 1048576 | tf_op jit(solution)/shard_map/all_to_all | solution.py:162
  77.6 0.8 shard_map.106
  78.4 16.0 %all-to-all-start.2 = ((bf16[32,16,128]{2,1,0:T(8,128)(2,1)}), bf16[32,16,128]{2,1,0:T(8,128)(2,1)S(1)}, u32[]{:S(2)}, u32[]{:S(2)}) async-start(bf16[32,16,128]{2,1,0:T(8,128)(2,1)} %shard_map.106), calls=%async_computation.2 | async-start | bytes 262144 | tf_op jit(solution)/shard_map/all_to_all | solution.py:162
  95.0 2.2 %collective-permute-start.3 = (bf16[1,2,256,512]{3,2,1,0:T(8,128)(2,1)S(1)}, bf16[1,2,256,512]{3,2,1,0:T(8,128)(2,1)}, u32[]{:S(2)}, u32[]{:S(2)}) collective-permute-start(bf16[1,2,256,512]{3,2,1,0:T(8,128)(2,1)S(1)} %shard_map.102), channel_id=1, source_target_pairs={{0,4},{1,5},{2,6},{3,7},{4,8},{5,9},{6,10},{7,11},{8,12},{9,13},{1... | collective-permute-start | bytes 1572872 | tf_op jit(solution)/shard_map/ppermute | solution.py:169
  97.2 0.6 shard_map.103
  97.8 3.7 %collective-permute-start.4 = (bf16[1,2,256,512]{3,2,1,0:T(8,128)(2,1)S(1)}, bf16[1,2,256,512]{3,2,1,0:T(8,128)(2,1)}, u32[]{:S(2)}, u32[]{:S(2)}) collective-permute-start(bf16[1,2,256,512]{3,2,1,0:T(8,128)(2,1)S(1)} %shard_map.103), channel_id=1, source_target_pairs={{0,8},{1,9},{2,10},{3,11},{4,12},{5,13},{6,14},{7,15},{8,0},{9,1},... | collective-permute-start | bytes 1572872 | tf_op jit(solution)/shard_map/ppermute | solution.py:169
  101.5 1.4 shard_map.104
  102.9 2.7 %collective-permute-start.5 = (bf16[1,2,256,512]{3,2,1,0:T(8,128)(2,1)}, bf16[1,2,256,512]{3,2,1,0:T(8,128)(2,1)}, u32[]{:S(2)}, u32[]{:S(2)}) collective-permute-start(bf16[1,2,256,512]{3,2,1,0:T(8,128)(2,1)} %shard_map.104), channel_id=1, source_target_pairs={{0,12},{1,13},{2,14},{3,15},{4,0},{5,1},{6,2},{7,3},{8,4},{9,5},{1... | collective-permute-start | bytes 1572872 | tf_op jit(solution)/shard_map/ppermute | solution.py:169
  105.6 0.7 fusion.2.rows_ref
  106.3 1.9 %shard_map.107 = bf16[32,16,128]{2,1,0:T(8,128)(2,1)} custom-call(s32[32]{0:T(128)S(1)} %bitcast.26, s32[16]{0:T(128)S(1)} %copy-done.7, s32[32,128]{1,0:T(8,128)S(1)} %fusion.2.rows_ref, bf16[32,16,128]{2,1,0:T(8,128)(2,1)S(1)} %all-to-all-done.2.v_ref), custom_call_target="tpu_custom_call" | custom-call | flops 33554432 | bytes 262144 | tf_op jit(solution)/shard_map/pallas_call | solution.py:146
  108.2 9.1 %all-to-all-start.3 = ((bf16[32,16,128]{2,1,0:T(8,128)(2,1)}), bf16[32,16,128]{2,1,0:T(8,128)(2,1)S(1)}, u32[]{:S(2)}, u32[]{:S(2)}) async-start(bf16[32,16,128]{2,1,0:T(8,128)(2,1)} %shard_map.107), calls=%async_computation.3 | async-start | bytes 262144 | tf_op jit(solution)/shard_map/all_to_all | solution.py:162
  117.9 0.8 copy-done.3
  118.7 7.5 %all-to-all-done.3.b_ref = bf16[32,16,128]{2,1,0:T(8,128)(2,1)S(1)} async-done(((bf16[32,16,128]{2,1,0:T(8,128)(2,1)}), bf16[32,16,128]{2,1,0:T(8,128)(2,1)S(1)}, u32[]{:S(2)}, u32[]{:S(2)}) %all-to-all-start.3) | async-done | bytes 131104 | tf_op jit(solution)/shard_map/all_to_all | solution.py:162
  126.3 13.1 %all-gather.1 = bf16[8,128,256]{2,1,0:T(8,128)(2,1)S(1)} all-gather(bf16[2,128,256]{2,1,0:T(8,128)(2,1)S(1)} %shard_map.108), channel_id=3, replica_groups={{0,1,2,3},{4,5,6,7},{8,9,10,11},{12,13,14,15},{16,17,18,19},{20,21,22,2..., dimensions={0}, use_global_device_ids=true | all-gather | bytes 655360 | tf_op jit(solution)/shard_map/all_gather | solution.py:173
  139.4 1.0 copy-done.4
  140.4 2.6 %shard_map.109 = (bf16[4,2,128,256]{3,2,1,0:T(8,128)(2,1)S(1)}, bf16[4,2,128,256]{3,2,1,0:T(8,128)(2,1)S(1)}) custom-call(s32[2]{0:T(128)S(1)} %pad_add_fusion.x_ref, bf16[1,2,256,512]{3,2,1,0:T(8,128)(2,1)S(1)} %copy-done.4, bf16[1,2,256,512]{3,2,1,0:T(8,128)(2,1)} %collective-permute-done.3.refs_1_, ...), custom_call_target="tpu_custom_call" | custom-call | flops 1073741824 | bytes 3670024 | tf_op jit(solution)/shard_map/pallas_call | solution.py:108
  143.1 4.4 %collective-permute-start.6 = (bf16[4,2,128,256]{3,2,1,0:T(8,128)(2,1)S(1)}, bf16[4,2,128,256]{3,2,1,0:T(8,128)(2,1)S(1)}, u32[]{:S(2)}, u32[]{:S(2)}) collective-permute-start(bf16[4,2,128,256]{3,2,1,0:T(8,128)(2,1)S(1)} %get-tuple-element.5), channel_id=1, source_target_pairs={{0,16},{16,0},{32,48},{48,32},{64,80},{80,64},{96,112},{112,96},{1... | collective-permute-start | bytes 1572872 | tf_op jit(solution)/shard_map/ppermute | solution.py:210
  147.5 1.5 collective-permute-done.6.b_ref
  149.2 12.1 %all_to_all.27.p_ref = bf16[4,2,128,256]{3,2,1,0:T(8,128)(2,1)S(1)} all-to-all(bf16[4,2,128,256]{3,2,1,0:T(8,128)(2,1)S(1)} %shard_map.110), channel_id=1, replica_groups={{0,4,8,12},{1,5,9,13},{2,6,10,14},{3,7,11,15},{16,20,24,28},{17,21,25,2..., dimensions={0} | all-to-all | bytes 1048576 | tf_op jit(solution)/shard_map/all_to_all | solution.py:162
  161.3 0.7 shard_map.111
  (29 shorter events, 3.3 us)
Async XLA Ops:
  0.7 1.2 copy-start.1
  2.0 1.2 copy-start.2
  3.8 29.1 %collective-permute-start = (bf16[2,2,128,512]{3,2,1,0:T(8,128)(2,1)S(1)}, bf16[2,2,128,512]{3,2,1,0:T(8,128)(2,1)S(1)}, u32[]{:S(2)}, u32[]{:S(2)}) collective-permute-start(bf16[2,2,128,512]{3,2,1,0:T(8,128)(2,1)S(1)} %shard_map.96), channel_id=1, source_target_pairs={{0,4},{1,5},{2,6},{3,7},{4,8},{5,9},{6,10},{7,11},{8,12},{9,13},{1... | collective-permute-start | bytes 1572872 | tf_op jit(solution)/shard_map/ppermute | solution.py:169
  8.3 8.8 %copy-start.8 = (bf16[1,2,128,256]{3,2,1,0:T(8,128)(2,1)S(1)}, bf16[1,2,128,256]{3,2,1,0:T(8,128)(2,1)}, u32[]{:S(2)}) copy-start(bf16[1,2,128,256]{3,2,1,0:T(8,128)(2,1)} %param.10) | copy-start | bytes 393220
  8.3 24.6 %collective-permute-start.1 = (bf16[2,2,128,512]{3,2,1,0:T(8,128)(2,1)S(1)}, bf16[2,2,128,512]{3,2,1,0:T(8,128)(2,1)S(1)}, u32[]{:S(2)}, u32[]{:S(2)}) collective-permute-start(bf16[2,2,128,512]{3,2,1,0:T(8,128)(2,1)S(1)} %shard_map.97), channel_id=1, source_target_pairs={{0,8},{1,9},{2,10},{3,11},{4,12},{5,13},{6,14},{7,15},{8,0},{9,1},... | collective-permute-start | bytes 1572872 | tf_op jit(solution)/shard_map/ppermute | solution.py:169
  13.4 19.5 %collective-permute-start.2 = (bf16[2,2,128,512]{3,2,1,0:T(8,128)(2,1)S(1)}, bf16[2,2,128,512]{3,2,1,0:T(8,128)(2,1)S(1)}, u32[]{:S(2)}, u32[]{:S(2)}) collective-permute-start(bf16[2,2,128,512]{3,2,1,0:T(8,128)(2,1)S(1)} %shard_map.98), channel_id=1, source_target_pairs={{0,12},{1,13},{2,14},{3,15},{4,0},{5,1},{6,2},{7,3},{8,4},{9,5},{1... | collective-permute-start | bytes 1572872 | tf_op jit(solution)/shard_map/ppermute | solution.py:169
  67.0 27.4 %copy-start = (bf16[1,2,256,2048]{3,2,1,0:T(8,128)(2,1)S(1)}, bf16[1,2,256,2048]{3,2,1,0:T(8,128)(2,1)}, u32[]{:S(2)}) copy-start(bf16[1,2,256,2048]{3,2,1,0:T(8,128)(2,1)} %param.11) | copy-start | bytes 6291460
  78.4 27.9 %all-to-all-start.2 = ((bf16[32,16,128]{2,1,0:T(8,128)(2,1)}), bf16[32,16,128]{2,1,0:T(8,128)(2,1)S(1)}, u32[]{:S(2)}, u32[]{:S(2)}) async-start(bf16[32,16,128]{2,1,0:T(8,128)(2,1)} %shard_map.106), calls=%async_computation.2 | async-start | bytes 262144 | tf_op jit(solution)/shard_map/all_to_all | solution.py:162
  95.0 11.4 %copy-start.6 = (s32[32,1]{0,1:T(1,128)S(1)}, s32[32,1]{0,1:T(1,128)}, u32[]{:S(2)}) copy-start(s32[32,1]{0,1:T(1,128)} %param.13) | copy-start | bytes 388
  95.0 11.3 %copy-start.7 = (s32[16]{0:T(128)S(1)}, s32[16]{0:T(128)}, u32[]{:S(2)}) copy-start(s32[16]{0:T(128)} %owner_ref.1) | copy-start | bytes 196
  95.0 44.4 %collective-permute-start.3 = (bf16[1,2,256,512]{3,2,1,0:T(8,128)(2,1)S(1)}, bf16[1,2,256,512]{3,2,1,0:T(8,128)(2,1)}, u32[]{:S(2)}, u32[]{:S(2)}) collective-permute-start(bf16[1,2,256,512]{3,2,1,0:T(8,128)(2,1)S(1)} %shard_map.102), channel_id=1, source_target_pairs={{0,4},{1,5},{2,6},{3,7},{4,8},{5,9},{6,10},{7,11},{8,12},{9,13},{1... | collective-permute-start | bytes 1572872 | tf_op jit(solution)/shard_map/ppermute | solution.py:169
  97.8 41.6 %collective-permute-start.4 = (bf16[1,2,256,512]{3,2,1,0:T(8,128)(2,1)S(1)}, bf16[1,2,256,512]{3,2,1,0:T(8,128)(2,1)}, u32[]{:S(2)}, u32[]{:S(2)}) collective-permute-start(bf16[1,2,256,512]{3,2,1,0:T(8,128)(2,1)S(1)} %shard_map.103), channel_id=1, source_target_pairs={{0,8},{1,9},{2,10},{3,11},{4,12},{5,13},{6,14},{7,15},{8,0},{9,1},... | collective-permute-start | bytes 1572872 | tf_op jit(solution)/shard_map/ppermute | solution.py:169
  102.9 23.3 %copy-start.5 = (bf16[1,2,128,256]{3,2,1,0:T(8,128)(2,1)S(1)}, bf16[1,2,128,256]{3,2,1,0:T(8,128)(2,1)}, u32[]{:S(2)}) copy-start(bf16[1,2,128,256]{3,2,1,0:T(8,128)(2,1)} %param.12) | copy-start | bytes 393220
  102.9 36.5 %collective-permute-start.5 = (bf16[1,2,256,512]{3,2,1,0:T(8,128)(2,1)}, bf16[1,2,256,512]{3,2,1,0:T(8,128)(2,1)}, u32[]{:S(2)}, u32[]{:S(2)}) collective-permute-start(bf16[1,2,256,512]{3,2,1,0:T(8,128)(2,1)} %shard_map.104), channel_id=1, source_target_pairs={{0,12},{1,13},{2,14},{3,15},{4,0},{5,1},{6,2},{7,3},{8,4},{9,5},{1... | collective-permute-start | bytes 1572872 | tf_op jit(solution)/shard_map/ppermute | solution.py:169
  108.2 17.9 %all-to-all-start.3 = ((bf16[32,16,128]{2,1,0:T(8,128)(2,1)}), bf16[32,16,128]{2,1,0:T(8,128)(2,1)S(1)}, u32[]{:S(2)}, u32[]{:S(2)}) async-start(bf16[32,16,128]{2,1,0:T(8,128)(2,1)} %shard_map.107), calls=%async_computation.3 | async-start | bytes 262144 | tf_op jit(solution)/shard_map/all_to_all | solution.py:162
  117.9 0.8 copy-start.3
  139.4 1.0 copy-start.4
  143.1 6.0 %collective-permute-start.6 = (bf16[4,2,128,256]{3,2,1,0:T(8,128)(2,1)S(1)}, bf16[4,2,128,256]{3,2,1,0:T(8,128)(2,1)S(1)}, u32[]{:S(2)}, u32[]{:S(2)}) collective-permute-start(bf16[4,2,128,256]{3,2,1,0:T(8,128)(2,1)S(1)} %get-tuple-element.5), channel_id=1, source_target_pairs={{0,16},{16,0},{32,48},{48,32},{64,80},{80,64},{96,112},{112,96},{1... | collective-permute-start | bytes 1572872 | tf_op jit(solution)/shard_map/ppermute | solution.py:210
where the time goes:
time: 164 us; the launch traced here: 162 us
  blocking collectives  82.5 us (50%)
  starting transfers between devices  49.5 us (30%)
  Pallas kernels  15 us (9%)
  waiting for transfers between devices  9.01 us (5%)
  local copies, waits for them, and re-layouts  4.3 us (3%)
    all_gather x3, blocking collectives, along_y(): lax.all_gather(block, 'blk', axis=0, tiled=False, axis_index_groups=ALONG_Y)  48.7 us
    all_to_all x3, blocking collectives, over(): lax.all_to_all(blocks, axis, 0, 0, axis_index_groups=groups, tiled=True)  33.8 us
    all_to_all x2, starting transfers between devices, over(): lax.all_to_all(blocks, axis, 0, 0, axis_index_groups=groups, tiled=True)  25 us
    ppermute x6, starting transfers between devices, shifted(): return lax.ppermute(block, 'blk', pairs)  20 us
    pallas_call x8, Pallas kernels, local(): pl.pallas_call(kernel, out_shape=shapes if len(shapes) > 1 else shapes[0]...  7.59 us
    all_to_all x2, waiting for transfers between devices, over(): lax.all_to_all(blocks, axis, 0, 0, axis_index_groups=groups, tiled=True)  7.48 us
    pallas_call x8, Pallas kernels, column_slice(): pl.pallas_call(slice_kernel, out_shape=jax.ShapeDtypeStruct(out, BF16), g...  5.49 us
    ppermute x1, starting transfers between devices, per_device(): taken = lax.ppermute(given, 'grp', [(i, i ^ 1) for i in range(GROUPS)])  4.43 us
  transfers between devices with their start and end apart: 9, of which 2 were waited for; matrix products, arithmetic and copies ran while one was open for 0% of the time, Pallas kernels for 4%

commit v1 on v0

--- a/solution.py
+++ b/solution.py
@@ -1,5 +1,3 @@
-import functools
-
 import jax
 import jax.numpy as jnp
 from jax import lax
@@ -13,6 +11,7 @@
 GROUPS = 32
 SIDE = 4
 LIMIT = 12 << 20
+STEPS = 1
 VM = pl.BlockSpec(memory_space=pltpu.VMEM)
 SM = pl.BlockSpec(memory_space=pltpu.SMEM)
 
@@ -30,17 +29,22 @@
     return with_real[:rows] - with_imag[rows:], with_imag[:rows] + with_real[rows:]
 
 
-def slice_kernel(x_ref, *refs):
-    *m_refs, o_ref = refs
-    for which, m_ref in enumerate(m_refs):
-        o_ref[which] = m_ref[...]
-
-
-def child_kernel(which, x_ref, *refs):
-    *m_refs, g_ref, o_ref = refs
-    for shift, m_ref in enumerate(m_refs):
-        block = lax.rem(x_ref[0] + SIDE - shift, SIDE)
-        for part, value in enumerate(products(m_ref[which], g_ref)):
+def shift_kernel(x_ref, m_ref, *o_refs):
+    inner = o_refs[0].shape[2]
+    for shift, o_ref in enumerate(o_refs):
+        first = lax.rem(x_ref[0] + shift, SIDE) * inner
+        o_ref[...] = m_ref[:, :, pl.ds(pl.multiple_of(first, inner), inner)]
+
+
+def split_kernel(m_ref, o_ref):
+    inner = o_ref.shape[3]
+    for block in range(SIDE):
+        o_ref[block] = m_ref[:, :, block * inner : (block + 1) * inner]
+
+
+def child_kernel(m_ref, g_ref, o_ref):
+    for block in range(SIDE):
+        for part, value in enumerate(products(m_ref[block], g_ref)):
             o_ref[block, part] = value.astype(BF16)
 
 
@@ -50,7 +54,7 @@
     half = x_ref[1]
     for shift, m_ref in enumerate(m_refs):
         block = lax.rem(x_ref[0] + SIDE - shift, SIDE)
-        for part, value in enumerate(products(m_ref[0], g_ref)):
+        for part, value in enumerate(products(m_ref[...], g_ref)):
             top, low = value[:rows], value[rows:]
             kept_ref[block, part] = jnp.where(half == 0, top, low).astype(BF16)
             given_ref[block, part] = jnp.where(half == 0, low, top).astype(BF16)
@@ -72,9 +76,11 @@
     o_ref[...] = wide.astype(BF16).reshape(o_ref.shape)
 
 
-def total_kernel(p_ref, o_ref):
+def total_kernel(p_ref, *o_refs):
     for part in range(2):
-        o_ref[part] = total(p_ref, part).astype(BF16)
+        value = total(p_ref, part).astype(BF16)
+        for o_ref in o_refs:
+            o_ref[part] = value
 
 
 def route_kernel(parent_ref, owner_ref, rows_ref, v_ref, o_ref, sums_ref):
@@ -115,30 +121,34 @@
     )(*operands)
 
 
-def column_slice(here, shift, *matrices):
-    rows, inner = matrices[0].shape[1:]
-    shape = (2, rows, inner // SIDE)
-    out = (len(matrices),) + shape
-    return pl.pallas_call(
-        slice_kernel,
-        out_shape=jax.ShapeDtypeStruct(out, BF16),
+def shifted_columns(here, matrix):
+    rows, inner = matrix.shape[1:]
+    step = rows // STEPS
+    piece = (2, step, inner // SIDE)
+    return pl.pallas_call(
+        shift_kernel,
+        out_shape=[jax.ShapeDtypeStruct((2, rows, inner // SIDE), BF16)] * SIDE,
         grid_spec=pltpu.PrefetchScalarGridSpec(
             num_scalar_prefetch=1,
-            grid=(1,),
-            in_specs=[
-                pl.BlockSpec(shape, lambda i, x: (0, 0, lax.rem(x[0] + shift, SIDE)))
-                for _ in matrices
-            ],
-            out_specs=pl.BlockSpec(out, lambda i, x: (0, 0, 0, 0)),
+            grid=(STEPS,),
+            in_specs=[pl.BlockSpec((2, step, inner), lambda i, x: (0, i, 0))],
+            out_specs=[pl.BlockSpec(piece, lambda i, x: (0, i, 0))] * SIDE,
         ),
-        cost_estimate=cost(0, 4 * len(matrices) * shape[0] * shape[1] * shape[2]),
-        compiler_params=pltpu.CompilerParams(vmem_limit_bytes=LIMIT),
-    )(here, *matrices)
-
-
-def redistributed(here, *matrices):
-    moved = [shifted(column_slice(here, k, *matrices), k) for k in range(1, SIDE)]
-    return [column_slice(here, 0, *matrices)] + moved
+        cost_estimate=cost(0, 8 * rows * inner),
+    )(here, matrix)
+
+
+def column_blocks(matrix):
+    rows, inner = matrix.shape[1:]
+    step = rows // STEPS
+    return pl.pallas_call(
+        split_kernel,
+        out_shape=jax.ShapeDtypeStruct((SIDE, 2, rows, inner // SIDE), BF16),
+        grid=(STEPS,),
+        in_specs=[pl.BlockSpec((2, step, inner), lambda i: (0, i, 0))],
+        out_specs=pl.BlockSpec((SIDE, 2, step, inner // SIDE), lambda i: (0, 0, i, 0)),
+        cost_estimate=cost(0, 8 * rows * inner),
+    )(matrix)
 
 
 def route(parent_of, owner, rows_of, pieces):
@@ -191,16 +201,22 @@
     rows_of = (local_map // half_order) * rows + local_map % rows
     here = jnp.stack([slot_index // SIDE, group_index % 2]).astype(jnp.int32)
 
-    child = redistributed(here, child_inverse[0], border_block[0])
+    inverse = along_x(column_blocks(child_inverse[0]))
     source = along_y(child_rhs[0])
-    parts = local(functools.partial(child_kernel, 0), [fan], flops, here, *child, source, scalars=1)
+    parts = local(child_kernel, [fan], flops, inverse, source)
     parts = along_x(parts)
-    solved = local(total_kernel, [block], 0, parts)
-    source = along_y(solved)
-    parts = local(functools.partial(child_kernel, 1), [fan], flops, here, *child, source, scalars=1)
+    solved, sent = local(total_kernel, [block] * 2, 0, parts)
+    source = along_y(sent)
+    border, solved = lax.optimization_barrier((column_blocks(border_block[0]), solved))
+    border = along_x(border)
+    parts = local(child_kernel, [fan], flops, border, source)
     parts = along_x(parts)
+    parent = shifted_columns(here, parent_inverse[0])
+    parts, *parent = lax.optimization_barrier((parts, *parent))
     pieces = local(pieces_kernel, [(GROUPS, 2 * cols // GROUPS, rows)], 0, parts)
-    parent = redistributed(here, parent_inverse[0])
+    parent[2] = shifted(parent[2], 2)
+    parent[1] = shifted(parent[1], 1)
+    parent[3] = shifted(parent[3], 3)
     columns = over(pieces, "grp")
     sums = route(parent_of[:, 0], owner, rows_of, columns)
     sums = over(sums, "grp")

time: 164 us -> 154 us (0.939)
  blocking collectives: 82.5 us -> 72.1 us
  local copies, waits for them, and re-layouts: 4.3 us -> 0.02 us
  starting transfers between devices: 49.5 us -> 52.8 us
  Pallas kernels: 15 us -> 17 us
    all_to_all x2 -> x5, starting transfers between devices: 25 us -> 37.7 us  [over(): lax.all_to_all(blocks, axis, 0, 0, axis_index_groups=groups, tiled=True)]
    ppermute x6 -> x3, starting transfers between devices: 20 us -> 8.41 us  [shifted(): return lax.ppermute(block, 'blk', pairs)]
    all_gather x3, blocking collectives: 48.7 us -> 42.2 us  [along_y(): lax.all_gather(block, 'blk', axis=0, tiled=False, axis_index_groups=ALONG_Y)]
    unnamed x18 -> x12, local copies, waits for them, and re-layouts: 4.3 us -> 0.02 us
    all_to_all x3 -> x2, blocking collectives: 33.8 us -> 29.9 us  [over(): lax.all_to_all(blocks, axis, 0, 0, axis_index_groups=groups, tiled=True)]
    pallas_call x8 -> x3, Pallas kernels: 5.49 us -> 8.51 us  [the longest x2 4.64 us: column_blocks(): pl.pallas_call(split_kernel, out_shape=jax.ShapeDtypeStruct((SIDE, 2, row...]
    ppermute x1, starting transfers between devices: 4.43 us -> 6.67 us  [per_device(): taken = lax.ppermute(given, 'grp', [(i, i ^ 1) for i in range(GROUPS)])]
    all_to_all x2 -> x5, waiting for transfers between devices: 7.48 us -> 7.1 us  [over(): lax.all_to_all(blocks, axis, 0, 0, axis_index_groups=groups, tiled=True)]
  transfers between devices with their start and end apart: 9 -> 9, of which waited for: 2 -> 3; matrix products, arithmetic and copies ran while one was open for 0% -> 1% of each run, Pallas kernels for 4% -> 5%
where the time goes in v1:
time: 154 us; the launch traced here: 153 us
  blocking collectives  72.1 us (47%)
  starting transfers between devices  52.8 us (34%)
  Pallas kernels  17 us (11%)
  waiting for transfers between devices  8.62 us (6%)
    all_gather x3, blocking collectives, along_y(): lax.all_gather(block, 'blk', axis=0, tiled=False, axis_index_groups=ALONG_Y)  42.2 us
    all_to_all x5, starting transfers between devices, over(): lax.all_to_all(blocks, axis, 0, 0, axis_index_groups=groups, tiled=True)  37.7 us
    all_to_all x2, blocking collectives, over(): lax.all_to_all(blocks, axis, 0, 0, axis_index_groups=groups, tiled=True)  29.9 us
    ppermute x3, starting transfers between devices, shifted(): return lax.ppermute(block, 'blk', pairs)  8.41 us
    pallas_call x8, Pallas kernels, local(): pl.pallas_call(kernel, out_shape=shapes if len(shapes) > 1 else shapes[0]...  7.31 us
    all_to_all x5, waiting for transfers between devices, over(): lax.all_to_all(blocks, axis, 0, 0, axis_index_groups=groups, tiled=True)  7.1 us
    ppermute x1, starting transfers between devices, per_device(): taken = lax.ppermute(given, 'grp', [(i, i ^ 1) for i in range(GROUPS)])  6.67 us
    pallas_call x2, Pallas kernels, column_blocks(): pl.pallas_call(split_kernel, out_shape=jax.ShapeDtypeStruct((SIDE, 2, row...  4.64 us
  transfers between devices with their start and end apart: 9, of which 3 were waited for; matrix products, arithmetic and copies ran while one was open for 1% of the time, Pallas kernels for 5%

profile of v1, /device:TPU:1, one launch (start us, length us, event | category | flops | bytes accessed | tf_op | source)
XLA Modules:
  0.0 152.7 jit_solution(10008177123890610243)
XLA Ops:
  0.6 2.3 %shard_map.96 = bf16[4,2,128,512]{3,2,1,0:T(8,128)(2,1)} custom-call(bf16[2,128,2048]{2,1,0:T(8,128)(2,1)} %bitcast.16), custom_call_target="tpu_custom_call" | custom-call | bytes 2097152 | tf_op jit(solution)/shard_map/pallas_call | solution.py:144
  3.0 4.8 %all-to-all-start = ((bf16[4,2,128,512]{3,2,1,0:T(8,128)(2,1)}), bf16[4,2,128,512]{3,2,1,0:T(8,128)(2,1)S(1)}, u32[]{:S(2)}, u32[]{:S(2)}) async-start(bf16[4,2,128,512]{3,2,1,0:T(8,128)(2,1)} %shard_map.96), calls=%async_computation | async-start | bytes 2097152 | tf_op jit(solution)/shard_map/all_to_all | solution.py:172
  7.8 16.0 %all_gather.15.g_ref = bf16[4,2,128,256]{3,2,1,0:T(8,128)(2,1)S(1)} all-gather(bf16[1,2,128,256]{3,2,1,0:T(8,128)(2,1)S(1)} %copy-done.5), channel_id=1, replica_groups={{0,1,2,3},{4,5,6,7},{8,9,10,11},{12,13,14,15},{16,17,18,19},{20,21,22,2..., dimensions={0}, use_global_device_ids=true | all-gather | bytes 655360 | tf_op jit(solution)/shard_map/all_gather | solution.py:183
  23.8 1.5 shard_map.97
  25.3 4.4 %all-to-all-start.1 = ((bf16[4,2,128,256]{3,2,1,0:T(8,128)(2,1)}), bf16[4,2,128,256]{3,2,1,0:T(8,128)(2,1)S(1)}, u32[]{:S(2)}, u32[]{:S(2)}) async-start(bf16[4,2,128,256]{3,2,1,0:T(8,128)(2,1)} %shard_map.97), calls=%async_computation.1 | async-start | bytes 1048576 | tf_op jit(solution)/shard_map/all_to_all | solution.py:172
  29.7 2.3 %shard_map.95 = bf16[4,2,128,512]{3,2,1,0:T(8,128)(2,1)} custom-call(bf16[2,128,2048]{2,1,0:T(8,128)(2,1)} %bitcast.17), custom_call_target="tpu_custom_call" | custom-call | bytes 2097152 | tf_op jit(solution)/shard_map/pallas_call | solution.py:144
  32.0 4.6 %all-to-all-done.1.p_ref = bf16[4,2,128,256]{3,2,1,0:T(8,128)(2,1)S(1)} async-done(((bf16[4,2,128,256]{3,2,1,0:T(8,128)(2,1)}), bf16[4,2,128,256]{3,2,1,0:T(8,128)(2,1)S(1)}, u32[]{:S(2)}, u32[]{:S(2)}) %all-to-all-start.1) | async-done | bytes 524320 | tf_op jit(solution)/shard_map/all_to_all | solution.py:172
  36.7 0.7 shard_map.98
  37.4 3.5 %all-to-all-start.2 = ((bf16[4,2,128,512]{3,2,1,0:T(8,128)(2,1)}), bf16[4,2,128,512]{3,2,1,0:T(8,128)(2,1)S(1)}, u32[]{:S(2)}, u32[]{:S(2)}) async-start(bf16[4,2,128,512]{3,2,1,0:T(8,128)(2,1)} %shard_map.95), calls=%async_computation.2 | async-start | bytes 2097152 | tf_op jit(solution)/shard_map/all_to_all | solution.py:172
  40.9 13.7 %all-gather = bf16[8,128,256]{2,1,0:T(8,128)(2,1)S(1)} all-gather(bf16[2,128,256]{2,1,0:T(8,128)(2,1)S(1)} %get-tuple-element.20), channel_id=2, replica_groups={{0,1,2,3},{4,5,6,7},{8,9,10,11},{12,13,14,15},{16,17,18,19},{20,21,22,2..., dimensions={0}, use_global_device_ids=true | all-gather | bytes 655360 | tf_op jit(solution)/shard_map/all_gather | solution.py:183
  54.6 0.0 all-to-all-done.2.m_ref
  54.6 1.5 shard_map.99
  56.2 4.4 %all-to-all-start.3 = ((bf16[4,2,128,256]{3,2,1,0:T(8,128)(2,1)}), bf16[4,2,128,256]{3,2,1,0:T(8,128)(2,1)S(1)}, u32[]{:S(2)}, u32[]{:S(2)}) async-start(bf16[4,2,128,256]{3,2,1,0:T(8,128)(2,1)} %shard_map.99), calls=%async_computation.3 | async-start | bytes 1048576 | tf_op jit(solution)/shard_map/all_to_all | solution.py:172
  60.5 0.6 pad_add_fusion.x_ref
  61.1 3.9 %shard_map.100 = (bf16[2,256,512]{2,1,0:T(8,128)(2,1)}, bf16[2,256,512]{2,1,0:T(8,128)(2,1)}, bf16[2,256,512]{2,1,0:T(8,128)(2,1)}, bf16[2,256,512]{2,1,0:T(8,128)(2,1)}) custom-call(s32[2]{0:T(128)} %pad_add_fusion.x_ref, bf16[2,256,2048]{2,1,0:T(8,128)(2,1)} %bitcast.15), custom_call_target="tpu_custom_call" | custom-call | bytes 4194304 | tf_op jit(solution)/shard_map/pallas_call | solution.py:128
  65.0 2.5 %all-to-all-done.3.p_ref = bf16[4,2,128,256]{3,2,1,0:T(8,128)(2,1)S(1)} async-done(((bf16[4,2,128,256]{3,2,1,0:T(8,128)(2,1)}), bf16[4,2,128,256]{3,2,1,0:T(8,128)(2,1)S(1)}, u32[]{:S(2)}, u32[]{:S(2)}) %all-to-all-start.3) | async-done | bytes 524320 | tf_op jit(solution)/shard_map/all_to_all | solution.py:172
  67.5 0.8 shard_map.101
  68.3 20.5 %all-to-all-start.4 = ((bf16[32,16,128]{2,1,0:T(8,128)(2,1)}), bf16[32,16,128]{2,1,0:T(8,128)(2,1)S(1)}, u32[]{:S(2)}, u32[]{:S(2)}) async-start(bf16[32,16,128]{2,1,0:T(8,128)(2,1)} %shard_map.101), calls=%async_computation.4 | async-start | bytes 262144 | tf_op jit(solution)/shard_map/all_to_all | solution.py:172
  88.8 2.2 %collective-permute-start = (bf16[2,256,512]{2,1,0:T(8,128)(2,1)}, bf16[2,256,512]{2,1,0:T(8,128)(2,1)S(1)}, u32[]{:S(2)}, u32[]{:S(2)}) collective-permute-start(bf16[2,256,512]{2,1,0:T(8,128)(2,1)} %get-tuple-element.26), channel_id=1, source_target_pairs={{0,4},{1,5},{2,6},{3,7},{4,8},{5,9},{6,10},{7,11},{8,12},{9,13},{1... | collective-permute-start | bytes 1572872 | tf_op jit(solution)/shard_map/ppermute | solution.py:179
  91.0 3.7 %collective-permute-start.1 = (bf16[2,256,512]{2,1,0:T(8,128)(2,1)}, bf16[2,256,512]{2,1,0:T(8,128)(2,1)S(1)}, u32[]{:S(2)}, u32[]{:S(2)}) collective-permute-start(bf16[2,256,512]{2,1,0:T(8,128)(2,1)} %get-tuple-element.27), channel_id=1, source_target_pairs={{0,8},{1,9},{2,10},{3,11},{4,12},{5,13},{6,14},{7,15},{8,0},{9,1},... | collective-permute-start | bytes 1572872 | tf_op jit(solution)/shard_map/ppermute | solution.py:179
  94.7 2.5 %collective-permute-start.2 = (bf16[2,256,512]{2,1,0:T(8,128)(2,1)}, bf16[2,256,512]{2,1,0:T(8,128)(2,1)S(1)}, u32[]{:S(2)}, u32[]{:S(2)}) collective-permute-start(bf16[2,256,512]{2,1,0:T(8,128)(2,1)} %get-tuple-element.28), channel_id=1, source_target_pairs={{0,12},{1,13},{2,14},{3,15},{4,0},{5,1},{6,2},{7,3},{8,4},{9,5},{1... | collective-permute-start | bytes 1572872 | tf_op jit(solution)/shard_map/ppermute | solution.py:179
  97.3 0.7 fusion.2.rows_ref
  98.0 1.2 shard_map.102
  99.3 17.5 %all_to_all.35.b_ref = bf16[32,16,128]{2,1,0:T(8,128)(2,1)S(1)} all-to-all(bf16[32,16,128]{2,1,0:T(8,128)(2,1)S(1)} %shard_map.102), channel_id=1, replica_groups=mesh['grp'=32,'blk'=16] {'grp'}, dimensions={0} | all-to-all | bytes 262144 | tf_op jit(solution)/shard_map/all_to_all | solution.py:172
  116.8 0.1 shard_map.103
  116.9 12.5 %all-gather.1 = bf16[8,128,256]{2,1,0:T(8,128)(2,1)S(1)} all-gather(bf16[2,128,256]{2,1,0:T(8,128)(2,1)S(1)} %shard_map.103), channel_id=3, replica_groups={{0,1,2,3},{4,5,6,7},{8,9,10,11},{12,13,14,15},{16,17,18,19},{20,21,22,2..., dimensions={0}, use_global_device_ids=true | all-gather | bytes 655360 | tf_op jit(solution)/shard_map/all_gather | solution.py:183
  129.5 1.8 %shard_map.104 = (bf16[4,2,128,256]{3,2,1,0:T(8,128)(2,1)S(1)}, bf16[4,2,128,256]{3,2,1,0:T(8,128)(2,1)S(1)}) custom-call(s32[2]{0:T(128)S(1)} %copy-done.3, bf16[2,256,512]{2,1,0:T(8,128)(2,1)S(1)} %copy-done.4, bf16[2,256,512]{2,1,0:T(8,128)(2,1)S(1)} %collective-permute-done.refs_1_, bf16[2,256,512]{2,1,0:T(8,128)(2,1)S(1)} %collective-permute-done.1.refs_2_, ...), custom_call_target="tpu_custom_call" | custom-call | flops 1073741824 | bytes 3670024 | tf_op jit(solution)/shard_map/pallas_call | solution.py:114
  131.3 6.7 %collective-permute-start.3 = (bf16[4,2,128,256]{3,2,1,0:T(8,128)(2,1)S(1)}, bf16[4,2,128,256]{3,2,1,0:T(8,128)(2,1)S(1)}, u32[]{:S(2)}, u32[]{:S(2)}) collective-permute-start(bf16[4,2,128,256]{3,2,1,0:T(8,128)(2,1)S(1)} %get-tuple-element.31), channel_id=1, source_target_pairs={{0,16},{16,0},{32,48},{48,32},{64,80},{80,64},{96,112},{112,96},{1... | collective-permute-start | bytes 1572872 | tf_op jit(solution)/shard_map/ppermute | solution.py:226
  138.0 1.5 collective-permute-done.3.b_ref
  139.5 0.1 shard_map.105
  139.6 12.3 %all_to_all.36.p_ref = bf16[4,2,128,256]{3,2,1,0:T(8,128)(2,1)S(1)} all-to-all(bf16[4,2,128,256]{3,2,1,0:T(8,128)(2,1)S(1)} %shard_map.105), channel_id=1, replica_groups={{0,4,8,12},{1,5,9,13},{2,6,10,14},{3,7,11,15},{16,20,24,28},{17,21,25,2..., dimensions={0} | all-to-all | bytes 1048576 | tf_op jit(solution)/shard_map/all_to_all | solution.py:172
  151.9 0.7 shard_map.106
  (17 shorter events, 0.0 us)
Async XLA Ops:
  0.6 7.2 %copy-start.5 = (bf16[1,2,128,256]{3,2,1,0:T(8,128)(2,1)S(1)}, bf16[1,2,128,256]{3,2,1,0:T(8,128)(2,1)}, u32[]{:S(2)}) copy-start(bf16[1,2,128,256]{3,2,1,0:T(8,128)(2,1)} %param.10) | copy-start | bytes 393220
  3.0 20.8 %all-to-all-start = ((bf16[4,2,128,512]{3,2,1,0:T(8,128)(2,1)}), bf16[4,2,128,512]{3,2,1,0:T(8,128)(2,1)S(1)}, u32[]{:S(2)}, u32[]{:S(2)}) async-start(bf16[4,2,128,512]{3,2,1,0:T(8,128)(2,1)} %shard_map.96), calls=%async_computation | async-start | bytes 2097152 | tf_op jit(solution)/shard_map/all_to_all | solution.py:172
  25.3 11.4 %all-to-all-start.1 = ((bf16[4,2,128,256]{3,2,1,0:T(8,128)(2,1)}), bf16[4,2,128,256]{3,2,1,0:T(8,128)(2,1)S(1)}, u32[]{:S(2)}, u32[]{:S(2)}) async-start(bf16[4,2,128,256]{3,2,1,0:T(8,128)(2,1)} %shard_map.97), calls=%async_computation.1 | async-start | bytes 1048576 | tf_op jit(solution)/shard_map/all_to_all | solution.py:172
  37.4 17.2 %all-to-all-start.2 = ((bf16[4,2,128,512]{3,2,1,0:T(8,128)(2,1)}), bf16[4,2,128,512]{3,2,1,0:T(8,128)(2,1)S(1)}, u32[]{:S(2)}, u32[]{:S(2)}) async-start(bf16[4,2,128,512]{3,2,1,0:T(8,128)(2,1)} %shard_map.95), calls=%async_computation.2 | async-start | bytes 2097152 | tf_op jit(solution)/shard_map/all_to_all | solution.py:172
  56.2 41.8 %copy-start.1 = (s32[32,1]{0,1:T(1,128)S(1)}, s32[32,1]{0,1:T(1,128)}, u32[]{:S(2)}) copy-start(s32[32,1]{0,1:T(1,128)} %param.13) | copy-start | bytes 388
  56.2 41.9 %copy-start.2 = (s32[16]{0:T(128)S(1)}, s32[16]{0:T(128)}, u32[]{:S(2)}) copy-start(s32[16]{0:T(128)} %owner_ref.1) | copy-start | bytes 196
  56.2 11.3 %all-to-all-start.3 = ((bf16[4,2,128,256]{3,2,1,0:T(8,128)(2,1)}), bf16[4,2,128,256]{3,2,1,0:T(8,128)(2,1)S(1)}, u32[]{:S(2)}, u32[]{:S(2)}) async-start(bf16[4,2,128,256]{3,2,1,0:T(8,128)(2,1)} %shard_map.99), calls=%async_computation.3 | async-start | bytes 1048576 | tf_op jit(solution)/shard_map/all_to_all | solution.py:172
  60.5 56.3 %copy-start = (bf16[1,2,128,256]{3,2,1,0:T(8,128)(2,1)S(1)}, bf16[1,2,128,256]{3,2,1,0:T(8,128)(2,1)}, u32[]{:S(2)}) copy-start(bf16[1,2,128,256]{3,2,1,0:T(8,128)(2,1)} %param.12) | copy-start | bytes 393220
  61.1 68.3 %copy-start.3 = (s32[2]{0:T(128)S(1)}, s32[2]{0:T(128)}, u32[]{:S(2)}) copy-start(s32[2]{0:T(128)} %pad_add_fusion.x_ref) | copy-start | bytes 28
  65.0 64.5 %copy-start.4 = (bf16[2,256,512]{2,1,0:T(8,128)(2,1)S(1)}, bf16[2,256,512]{2,1,0:T(8,128)(2,1)}, u32[]{:S(2)}) copy-start(bf16[2,256,512]{2,1,0:T(8,128)(2,1)} %get-tuple-element.25.refs_0_) | copy-start | bytes 1572868
  68.3 29.7 %all-to-all-start.4 = ((bf16[32,16,128]{2,1,0:T(8,128)(2,1)}), bf16[32,16,128]{2,1,0:T(8,128)(2,1)S(1)}, u32[]{:S(2)}, u32[]{:S(2)}) async-start(bf16[32,16,128]{2,1,0:T(8,128)(2,1)} %shard_map.101), calls=%async_computation.4 | async-start | bytes 262144 | tf_op jit(solution)/shard_map/all_to_all | solution.py:172
  88.8 40.6 %collective-permute-start = (bf16[2,256,512]{2,1,0:T(8,128)(2,1)}, bf16[2,256,512]{2,1,0:T(8,128)(2,1)S(1)}, u32[]{:S(2)}, u32[]{:S(2)}) collective-permute-start(bf16[2,256,512]{2,1,0:T(8,128)(2,1)} %get-tuple-element.26), channel_id=1, source_target_pairs={{0,4},{1,5},{2,6},{3,7},{4,8},{5,9},{6,10},{7,11},{8,12},{9,13},{1... | collective-permute-start | bytes 1572872 | tf_op jit(solution)/shard_map/ppermute | solution.py:179
  91.0 38.4 %collective-permute-start.1 = (bf16[2,256,512]{2,1,0:T(8,128)(2,1)}, bf16[2,256,512]{2,1,0:T(8,128)(2,1)S(1)}, u32[]{:S(2)}, u32[]{:S(2)}) collective-permute-start(bf16[2,256,512]{2,1,0:T(8,128)(2,1)} %get-tuple-element.27), channel_id=1, source_target_pairs={{0,8},{1,9},{2,10},{3,11},{4,12},{5,13},{6,14},{7,15},{8,0},{9,1},... | collective-permute-start | bytes 1572872 | tf_op jit(solution)/shard_map/ppermute | solution.py:179
  94.7 34.7 %collective-permute-start.2 = (bf16[2,256,512]{2,1,0:T(8,128)(2,1)}, bf16[2,256,512]{2,1,0:T(8,128)(2,1)S(1)}, u32[]{:S(2)}, u32[]{:S(2)}) collective-permute-start(bf16[2,256,512]{2,1,0:T(8,128)(2,1)} %get-tuple-element.28), channel_id=1, source_target_pairs={{0,12},{1,13},{2,14},{3,15},{4,0},{5,1},{6,2},{7,3},{8,4},{9,5},{1... | collective-permute-start | bytes 1572872 | tf_op jit(solution)/shard_map/ppermute | solution.py:179
  131.3 8.2 %collective-permute-start.3 = (bf16[4,2,128,256]{3,2,1,0:T(8,128)(2,1)S(1)}, bf16[4,2,128,256]{3,2,1,0:T(8,128)(2,1)S(1)}, u32[]{:S(2)}, u32[]{:S(2)}) collective-permute-start(bf16[4,2,128,256]{3,2,1,0:T(8,128)(2,1)S(1)} %get-tuple-element.31), channel_id=1, source_target_pairs={{0,16},{16,0},{32,48},{48,32},{64,80},{80,64},{96,112},{112,96},{1... | collective-permute-start | bytes 1572872 | tf_op jit(solution)/shard_map/ppermute | solution.py:226

commit v2 on v1

--- a/solution.py
+++ b/solution.py
@@ -1,3 +1,5 @@
+import functools
+
 import jax
 import jax.numpy as jnp
 from jax import lax
@@ -48,16 +50,15 @@
             o_ref[block, part] = value.astype(BF16)
 
 
-def parent_kernel(x_ref, *refs):
-    *m_refs, g_ref, kept_ref, given_ref = refs
-    rows = kept_ref.shape[2]
-    half = x_ref[1]
+def parent_kernel(own, x_ref, *refs):
+    *m_refs, g_ref, o_ref = refs
+    rows = o_ref.shape[2]
+    half = x_ref[1] if own else 1 - x_ref[1]
+    here = pl.ds(pl.multiple_of(half * rows, rows), rows)
     for shift, m_ref in enumerate(m_refs):
         block = lax.rem(x_ref[0] + SIDE - shift, SIDE)
-        for part, value in enumerate(products(m_ref[...], g_ref)):
-            top, low = value[:rows], value[rows:]
-            kept_ref[block, part] = jnp.where(half == 0, top, low).astype(BF16)
-            given_ref[block, part] = jnp.where(half == 0, low, top).astype(BF16)
+        for part, value in enumerate(products(m_ref[:, here, :], g_ref)):
+            o_ref[block, part] = value.astype(BF16)
 
 
 def joined_kernel(a_ref, b_ref, o_ref):
@@ -205,14 +206,14 @@
     source = along_y(child_rhs[0])
     parts = local(child_kernel, [fan], flops, inverse, source)
     parts = along_x(parts)
+    parent = shifted_columns(here, parent_inverse[0])
+    parts, *parent = lax.optimization_barrier((parts, *parent))
     solved, sent = local(total_kernel, [block] * 2, 0, parts)
     source = along_y(sent)
     border, solved = lax.optimization_barrier((column_blocks(border_block[0]), solved))
     border = along_x(border)
     parts = local(child_kernel, [fan], flops, border, source)
     parts = along_x(parts)
-    parent = shifted_columns(here, parent_inverse[0])
-    parts, *parent = lax.optimization_barrier((parts, *parent))
     pieces = local(pieces_kernel, [(GROUPS, 2 * cols // GROUPS, rows)], 0, parts)
     parent[2] = shifted(parent[2], 2)
     parent[1] = shifted(parent[1], 1)
@@ -222,7 +223,10 @@
     sums = over(sums, "grp")
     right = local(right_kernel, [block], 0, sums, parent_rhs[0])
     source = along_y(right)
-    kept, given = local(parent_kernel, [fan, fan], 2 * flops, here, *parent, source, scalars=1)
+    given, kept = (
+        local(functools.partial(parent_kernel, own), [fan], flops, here, *parent, source, scalars=1)
+        for own in (False, True)
+    )
     taken = lax.ppermute(given, "grp", [(i, i ^ 1) for i in range(GROUPS)])
     parts = local(joined_kernel, [fan], 0, kept, taken)
     parts = along_x(parts)

time: 154 us -> 152 us (0.987)
  blocking collectives: 72.1 us -> 84.5 us
  waiting for transfers between devices: 8.62 us -> 0.56 us
  starting transfers between devices: 52.8 us -> 47.1 us
    all_to_all x2 -> x3, blocking collectives: 29.9 us -> 40.9 us  [over(): lax.all_to_all(blocks, axis, 0, 0, axis_index_groups=groups, tiled=True)]
    all_to_all x5 -> x4, waiting for transfers between devices: 7.1 us -> 0.3 us  [over(): lax.all_to_all(blocks, axis, 0, 0, axis_index_groups=groups, tiled=True)]
    all_to_all x5 -> x4, starting transfers between devices: 37.7 us -> 33.1 us  [over(): lax.all_to_all(blocks, axis, 0, 0, axis_index_groups=groups, tiled=True)]
    pallas_call x8 -> x9, Pallas kernels: 7.31 us -> 7.19 us  [local(): pl.pallas_call(kernel, out_shape=shapes if len(shapes) > 1 else shapes[0]...]
  transfers between devices with their start and end apart: 9 -> 8, of which waited for: 3 -> 2; matrix products, arithmetic and copies ran while one was open for 1% -> 1% of each run, Pallas kernels for 5% -> 6%
where the time goes in v2:
time: 152 us; the launch traced here: 151 us
  blocking collectives  84.5 us (56%)
  starting transfers between devices  47.1 us (31%)
  Pallas kernels  16.7 us (11%)
    all_gather x3, blocking collectives, along_y(): lax.all_gather(block, 'blk', axis=0, tiled=False, axis_index_groups=ALONG_Y)  43.6 us
    all_to_all x3, blocking collectives, over(): lax.all_to_all(blocks, axis, 0, 0, axis_index_groups=groups, tiled=True)  40.9 us
    all_to_all x4, starting transfers between devices, over(): lax.all_to_all(blocks, axis, 0, 0, axis_index_groups=groups, tiled=True)  33.1 us
    ppermute x3, starting transfers between devices, shifted(): return lax.ppermute(block, 'blk', pairs)  8.41 us
    pallas_call x9, Pallas kernels, local(): pl.pallas_call(kernel, out_shape=shapes if len(shapes) > 1 else shapes[0]...  7.19 us
    ppermute x1, starting transfers between devices, per_device(): taken = lax.ppermute(given, 'grp', [(i, i ^ 1) for i in range(GROUPS)])  5.57 us
    pallas_call x2, Pallas kernels, column_blocks(): pl.pallas_call(split_kernel, out_shape=jax.ShapeDtypeStruct((SIDE, 2, row...  4.61 us
    pallas_call x1, Pallas kernels, shifted_columns(): pl.pallas_call(shift_kernel, out_shape=[jax.ShapeDtypeStruct((2, rows, in...  3.7 us
  transfers between devices with their start and end apart: 8, of which 2 were waited for; matrix products, arithmetic and copies ran while one was open for 1% of the time, Pallas kernels for 6%

profile of v2, /device:TPU:1, one launch (start us, length us, event | category | flops | bytes accessed | tf_op | source)
XLA Modules:
  0.0 151.1 jit_solution(4616349759151864767)
XLA Ops:
  0.6 2.3 %shard_map.96 = bf16[4,2,128,512]{3,2,1,0:T(8,128)(2,1)} custom-call(bf16[2,128,2048]{2,1,0:T(8,128)(2,1)} %bitcast.17), custom_call_target="tpu_custom_call" | custom-call | bytes 2097152 | tf_op jit(solution)/shard_map/pallas_call | solution.py:145
  3.0 4.8 %all-to-all-start = ((bf16[4,2,128,512]{3,2,1,0:T(8,128)(2,1)}), bf16[4,2,128,512]{3,2,1,0:T(8,128)(2,1)S(1)}, u32[]{:S(2)}, u32[]{:S(2)}) async-start(bf16[4,2,128,512]{3,2,1,0:T(8,128)(2,1)} %shard_map.96), calls=%async_computation | async-start | bytes 2097152 | tf_op jit(solution)/shard_map/all_to_all | solution.py:173
  7.8 16.0 %all_gather.15.g_ref = bf16[4,2,128,256]{3,2,1,0:T(8,128)(2,1)S(1)} all-gather(bf16[1,2,128,256]{3,2,1,0:T(8,128)(2,1)S(1)} %copy-done.5), channel_id=1, replica_groups={{0,1,2,3},{4,5,6,7},{8,9,10,11},{12,13,14,15},{16,17,18,19},{20,21,22,2..., dimensions={0}, use_global_device_ids=true | all-gather | bytes 655360 | tf_op jit(solution)/shard_map/all_gather | solution.py:184
  23.8 1.5 %shard_map.97 = bf16[4,2,128,256]{3,2,1,0:T(8,128)(2,1)} custom-call(bf16[4,2,128,512]{3,2,1,0:T(8,128)(2,1)S(1)} %all-to-all-done.m_ref, bf16[4,2,128,256]{3,2,1,0:T(8,128)(2,1)S(1)} %all_gather.15.g_ref), custom_call_target="tpu_custom_call" | custom-call | flops 536870912 | bytes 2097152 | tf_op jit(solution)/shard_map/pallas_call | solution.py:115
  25.3 4.4 %all-to-all-start.1 = ((bf16[4,2,128,256]{3,2,1,0:T(8,128)(2,1)}), bf16[4,2,128,256]{3,2,1,0:T(8,128)(2,1)S(1)}, u32[]{:S(2)}, u32[]{:S(2)}) async-start(bf16[4,2,128,256]{3,2,1,0:T(8,128)(2,1)} %shard_map.97), calls=%async_computation.1 | async-start | bytes 1048576 | tf_op jit(solution)/shard_map/all_to_all | solution.py:173
  29.7 2.3 %shard_map.95 = bf16[4,2,128,512]{3,2,1,0:T(8,128)(2,1)} custom-call(bf16[2,128,2048]{2,1,0:T(8,128)(2,1)} %bitcast.18), custom_call_target="tpu_custom_call" | custom-call | bytes 2097152 | tf_op jit(solution)/shard_map/pallas_call | solution.py:145
  32.0 0.7 pad_add_fusion.x_ref
  32.7 3.7 %shard_map.98 = (bf16[2,256,512]{2,1,0:T(8,128)(2,1)}, bf16[2,256,512]{2,1,0:T(8,128)(2,1)}, bf16[2,256,512]{2,1,0:T(8,128)(2,1)}, bf16[2,256,512]{2,1,0:T(8,128)(2,1)}) custom-call(s32[2]{0:T(128)} %pad_add_fusion.x_ref, bf16[2,256,2048]{2,1,0:T(8,128)(2,1)} %bitcast.16), custom_call_target="tpu_custom_call" | custom-call | bytes 4194304 | tf_op jit(solution)/shard_map/pallas_call | solution.py:129
  36.4 0.3 all-to-all-done.1.p_ref
  36.7 0.7 shard_map.99
  37.4 3.9 %all-to-all-start.2 = ((bf16[4,2,128,512]{3,2,1,0:T(8,128)(2,1)}), bf16[4,2,128,512]{3,2,1,0:T(8,128)(2,1)S(1)}, u32[]{:S(2)}, u32[]{:S(2)}) async-start(bf16[4,2,128,512]{3,2,1,0:T(8,128)(2,1)} %shard_map.95), calls=%async_computation.2 | async-start | bytes 2097152 | tf_op jit(solution)/shard_map/all_to_all | solution.py:173
  41.3 13.8 %all-gather = bf16[8,128,256]{2,1,0:T(8,128)(2,1)S(1)} all-gather(bf16[2,128,256]{2,1,0:T(8,128)(2,1)S(1)} %get-tuple-element.27), channel_id=2, replica_groups={{0,1,2,3},{4,5,6,7},{8,9,10,11},{12,13,14,15},{16,17,18,19},{20,21,22,2..., dimensions={0}, use_global_device_ids=true | all-gather | bytes 655360 | tf_op jit(solution)/shard_map/all_gather | solution.py:184
  55.2 0.0 copy-start.1
  55.2 0.7 shard_map.100
  55.9 10.9 %all_to_all.35.p_ref = bf16[4,2,128,256]{3,2,1,0:T(8,128)(2,1)S(1)} all-to-all(bf16[4,2,128,256]{3,2,1,0:T(8,128)(2,1)S(1)} %shard_map.100), channel_id=1, replica_groups={{0,4,8,12},{1,5,9,13},{2,6,10,14},{3,7,11,15},{16,20,24,28},{17,21,25,2..., dimensions={0} | all-to-all | bytes 1048576 | tf_op jit(solution)/shard_map/all_to_all | solution.py:173
  66.8 0.8 shard_map.101
  67.6 19.9 %all-to-all-start.4 = ((bf16[32,16,128]{2,1,0:T(8,128)(2,1)}), bf16[32,16,128]{2,1,0:T(8,128)(2,1)S(1)}, u32[]{:S(2)}, u32[]{:S(2)}) async-start(bf16[32,16,128]{2,1,0:T(8,128)(2,1)} %shard_map.101), calls=%async_computation.4 | async-start | bytes 262144 | tf_op jit(solution)/shard_map/all_to_all | solution.py:173
  87.5 2.2 %collective-permute-start = (bf16[2,256,512]{2,1,0:T(8,128)(2,1)}, bf16[2,256,512]{2,1,0:T(8,128)(2,1)S(1)}, u32[]{:S(2)}, u32[]{:S(2)}) collective-permute-start(bf16[2,256,512]{2,1,0:T(8,128)(2,1)} %get-tuple-element.23), channel_id=1, source_target_pairs={{0,4},{1,5},{2,6},{3,7},{4,8},{5,9},{6,10},{7,11},{8,12},{9,13},{1... | collective-permute-start | bytes 1572872 | tf_op jit(solution)/shard_map/ppermute | solution.py:180
  89.7 3.7 %collective-permute-start.1 = (bf16[2,256,512]{2,1,0:T(8,128)(2,1)S(1)}, bf16[2,256,512]{2,1,0:T(8,128)(2,1)S(1)}, u32[]{:S(2)}, u32[]{:S(2)}) collective-permute-start(bf16[2,256,512]{2,1,0:T(8,128)(2,1)S(1)} %copy-done.7), channel_id=1, source_target_pairs={{0,8},{1,9},{2,10},{3,11},{4,12},{5,13},{6,14},{7,15},{8,0},{9,1},... | collective-permute-start | bytes 1572872 | tf_op jit(solution)/shard_map/ppermute | solution.py:180
  93.4 2.5 %collective-permute-start.2 = (bf16[2,256,512]{2,1,0:T(8,128)(2,1)S(1)}, bf16[2,256,512]{2,1,0:T(8,128)(2,1)S(1)}, u32[]{:S(2)}, u32[]{:S(2)}) collective-permute-start(bf16[2,256,512]{2,1,0:T(8,128)(2,1)S(1)} %copy-done.6), channel_id=1, source_target_pairs={{0,12},{1,13},{2,14},{3,15},{4,0},{5,1},{6,2},{7,3},{8,4},{9,5},{1... | collective-permute-start | bytes 1572872 | tf_op jit(solution)/shard_map/ppermute | solution.py:180
  95.9 0.7 fusion.2.rows_ref
  96.7 1.2 shard_map.102
  98.0 17.7 %all_to_all.36.b_ref = bf16[32,16,128]{2,1,0:T(8,128)(2,1)S(1)} all-to-all(bf16[32,16,128]{2,1,0:T(8,128)(2,1)S(1)} %shard_map.102), channel_id=1, replica_groups=mesh['grp'=32,'blk'=16] {'grp'}, dimensions={0} | all-to-all | bytes 262144 | tf_op jit(solution)/shard_map/all_to_all | solution.py:173
  115.7 0.1 shard_map.103
  115.8 13.8 %all-gather.1 = bf16[8,128,256]{2,1,0:T(8,128)(2,1)S(1)} all-gather(bf16[2,128,256]{2,1,0:T(8,128)(2,1)S(1)} %shard_map.103), channel_id=3, replica_groups={{0,1,2,3},{4,5,6,7},{8,9,10,11},{12,13,14,15},{16,17,18,19},{20,21,22,2..., dimensions={0}, use_global_device_ids=true | all-gather | bytes 655360 | tf_op jit(solution)/shard_map/all_gather | solution.py:184
  129.7 1.3 shard_map.105
  130.9 5.6 %collective-permute-start.3 = (bf16[4,2,128,256]{3,2,1,0:T(8,128)(2,1)S(1)}, bf16[4,2,128,256]{3,2,1,0:T(8,128)(2,1)S(1)}, u32[]{:S(2)}, u32[]{:S(2)}) collective-permute-start(bf16[4,2,128,256]{3,2,1,0:T(8,128)(2,1)S(1)} %shard_map.105), channel_id=1, source_target_pairs={{0,16},{16,0},{32,48},{48,32},{64,80},{80,64},{96,112},{112,96},{1... | collective-permute-start | bytes 1572872 | tf_op jit(solution)/shard_map/ppermute | solution.py:230
  136.5 1.3 shard_map.104.a_ref
  137.8 0.3 collective-permute-done.3.b_ref
  138.0 0.1 shard_map.106
  138.1 12.3 %all_to_all.37.p_ref = bf16[4,2,128,256]{3,2,1,0:T(8,128)(2,1)S(1)} all-to-all(bf16[4,2,128,256]{3,2,1,0:T(8,128)(2,1)S(1)} %shard_map.106), channel_id=1, replica_groups={{0,4,8,12},{1,5,9,13},{2,6,10,14},{3,7,11,15},{16,20,24,28},{17,21,25,2..., dimensions={0} | all-to-all | bytes 1048576 | tf_op jit(solution)/shard_map/all_to_all | solution.py:173
  150.4 0.7 shard_map.107
  (21 shorter events, 0.0 us)
Async XLA Ops:
  0.6 7.2 %copy-start.5 = (bf16[1,2,128,256]{3,2,1,0:T(8,128)(2,1)S(1)}, bf16[1,2,128,256]{3,2,1,0:T(8,128)(2,1)}, u32[]{:S(2)}) copy-start(bf16[1,2,128,256]{3,2,1,0:T(8,128)(2,1)} %param.10) | copy-start | bytes 393220
  3.0 20.8 %all-to-all-start = ((bf16[4,2,128,512]{3,2,1,0:T(8,128)(2,1)}), bf16[4,2,128,512]{3,2,1,0:T(8,128)(2,1)S(1)}, u32[]{:S(2)}, u32[]{:S(2)}) async-start(bf16[4,2,128,512]{3,2,1,0:T(8,128)(2,1)} %shard_map.96), calls=%async_computation | async-start | bytes 2097152 | tf_op jit(solution)/shard_map/all_to_all | solution.py:173
  25.3 11.4 %all-to-all-start.1 = ((bf16[4,2,128,256]{3,2,1,0:T(8,128)(2,1)}), bf16[4,2,128,256]{3,2,1,0:T(8,128)(2,1)S(1)}, u32[]{:S(2)}, u32[]{:S(2)}) async-start(bf16[4,2,128,256]{3,2,1,0:T(8,128)(2,1)} %shard_map.97), calls=%async_computation.1 | async-start | bytes 1048576 | tf_op jit(solution)/shard_map/all_to_all | solution.py:173
  37.4 17.8 %all-to-all-start.2 = ((bf16[4,2,128,512]{3,2,1,0:T(8,128)(2,1)}), bf16[4,2,128,512]{3,2,1,0:T(8,128)(2,1)S(1)}, u32[]{:S(2)}, u32[]{:S(2)}) async-start(bf16[4,2,128,512]{3,2,1,0:T(8,128)(2,1)} %shard_map.95), calls=%async_computation.2 | async-start | bytes 2097152 | tf_op jit(solution)/shard_map/all_to_all | solution.py:173
  55.1 34.6 %copy-start.7 = (bf16[2,256,512]{2,1,0:T(8,128)(2,1)S(1)}, bf16[2,256,512]{2,1,0:T(8,128)(2,1)}, u32[]{:S(2)}) copy-start(bf16[2,256,512]{2,1,0:T(8,128)(2,1)} %get-tuple-element.24) | copy-start | bytes 1572868
  55.1 38.3 %copy-start.6 = (bf16[2,256,512]{2,1,0:T(8,128)(2,1)S(1)}, bf16[2,256,512]{2,1,0:T(8,128)(2,1)}, u32[]{:S(2)}) copy-start(bf16[2,256,512]{2,1,0:T(8,128)(2,1)} %get-tuple-element.25) | copy-start | bytes 1572868
  55.1 41.6 %copy-start.3 = (s32[32,1]{0,1:T(1,128)S(1)}, s32[32,1]{0,1:T(1,128)}, u32[]{:S(2)}) copy-start(s32[32,1]{0,1:T(1,128)} %param.13) | copy-start | bytes 388
  55.1 41.6 %copy-start.4 = (s32[16]{0:T(128)S(1)}, s32[16]{0:T(128)}, u32[]{:S(2)}) copy-start(s32[16]{0:T(128)} %owner_ref.1) | copy-start | bytes 196
  55.2 60.5 %copy-start.1 = (bf16[1,2,128,256]{3,2,1,0:T(8,128)(2,1)S(1)}, bf16[1,2,128,256]{3,2,1,0:T(8,128)(2,1)}, u32[]{:S(2)}) copy-start(bf16[1,2,128,256]{3,2,1,0:T(8,128)(2,1)} %param.12) | copy-start | bytes 393220
  55.9 73.8 %copy-start = (bf16[2,256,512]{2,1,0:T(8,128)(2,1)S(1)}, bf16[2,256,512]{2,1,0:T(8,128)(2,1)}, u32[]{:S(2)}) copy-start(bf16[2,256,512]{2,1,0:T(8,128)(2,1)} %get-tuple-element.22.refs_0_) | copy-start | bytes 1572868
  55.9 73.8 %copy-start.2 = (s32[2]{0:T(128)S(1)}, s32[2]{0:T(128)}, u32[]{:S(2)}) copy-start(s32[2]{0:T(128)} %pad_add_fusion.x_ref) | copy-start | bytes 28
  67.6 29.1 %all-to-all-start.4 = ((bf16[32,16,128]{2,1,0:T(8,128)(2,1)}), bf16[32,16,128]{2,1,0:T(8,128)(2,1)S(1)}, u32[]{:S(2)}, u32[]{:S(2)}) async-start(bf16[32,16,128]{2,1,0:T(8,128)(2,1)} %shard_map.101), calls=%async_computation.4 | async-start | bytes 262144 | tf_op jit(solution)/shard_map/all_to_all | solution.py:173
  87.5 42.1 %collective-permute-start = (bf16[2,256,512]{2,1,0:T(8,128)(2,1)}, bf16[2,256,512]{2,1,0:T(8,128)(2,1)S(1)}, u32[]{:S(2)}, u32[]{:S(2)}) collective-permute-start(bf16[2,256,512]{2,1,0:T(8,128)(2,1)} %get-tuple-element.23), channel_id=1, source_target_pairs={{0,4},{1,5},{2,6},{3,7},{4,8},{5,9},{6,10},{7,11},{8,12},{9,13},{1... | collective-permute-start | bytes 1572872 | tf_op jit(solution)/shard_map/ppermute | solution.py:180
  89.7 39.9 %collective-permute-start.1 = (bf16[2,256,512]{2,1,0:T(8,128)(2,1)S(1)}, bf16[2,256,512]{2,1,0:T(8,128)(2,1)S(1)}, u32[]{:S(2)}, u32[]{:S(2)}) collective-permute-start(bf16[2,256,512]{2,1,0:T(8,128)(2,1)S(1)} %copy-done.7), channel_id=1, source_target_pairs={{0,8},{1,9},{2,10},{3,11},{4,12},{5,13},{6,14},{7,15},{8,0},{9,1},... | collective-permute-start | bytes 1572872 | tf_op jit(solution)/shard_map/ppermute | solution.py:180
  93.4 36.2 %collective-permute-start.2 = (bf16[2,256,512]{2,1,0:T(8,128)(2,1)S(1)}, bf16[2,256,512]{2,1,0:T(8,128)(2,1)S(1)}, u32[]{:S(2)}, u32[]{:S(2)}) collective-permute-start(bf16[2,256,512]{2,1,0:T(8,128)(2,1)S(1)} %copy-done.6), channel_id=1, source_target_pairs={{0,12},{1,13},{2,14},{3,15},{4,0},{5,1},{6,2},{7,3},{8,4},{9,5},{1... | collective-permute-start | bytes 1572872 | tf_op jit(solution)/shard_map/ppermute | solution.py:180
  130.9 7.1 %collective-permute-start.3 = (bf16[4,2,128,256]{3,2,1,0:T(8,128)(2,1)S(1)}, bf16[4,2,128,256]{3,2,1,0:T(8,128)(2,1)S(1)}, u32[]{:S(2)}, u32[]{:S(2)}) collective-permute-start(bf16[4,2,128,256]{3,2,1,0:T(8,128)(2,1)S(1)} %shard_map.105), channel_id=1, source_target_pairs={{0,16},{16,0},{32,48},{48,32},{64,80},{80,64},{96,112},{112,96},{1... | collective-permute-start | bytes 1572872 | tf_op jit(solution)/shard_map/ppermute | solution.py:230

commit v3 on v2

--- a/solution.py
+++ b/solution.py
@@ -13,7 +13,6 @@
 GROUPS = 32
 SIDE = 4
 LIMIT = 12 << 20
-STEPS = 1
 VM = pl.BlockSpec(memory_space=pltpu.VMEM)
 SM = pl.BlockSpec(memory_space=pltpu.SMEM)
 
@@ -31,10 +30,11 @@
     return with_real[:rows] - with_imag[rows:], with_imag[:rows] + with_real[rows:]
 
 
-def shift_kernel(x_ref, m_ref, *o_refs):
+def shift_kernel(m_ref, *o_refs):
     inner = o_refs[0].shape[2]
+    column = lax.axis_index("blk") // SIDE
     for shift, o_ref in enumerate(o_refs):
-        first = lax.rem(x_ref[0] + shift, SIDE) * inner
+        first = lax.rem(column + shift, SIDE) * inner
         o_ref[...] = m_ref[:, :, pl.ds(pl.multiple_of(first, inner), inner)]
 
 
@@ -50,13 +50,14 @@
             o_ref[block, part] = value.astype(BF16)
 
 
-def parent_kernel(own, x_ref, *refs):
+def parent_kernel(own, *refs):
     *m_refs, g_ref, o_ref = refs
     rows = o_ref.shape[2]
-    half = x_ref[1] if own else 1 - x_ref[1]
+    column = lax.axis_index("blk") // SIDE
+    half = lax.rem(lax.axis_index("grp") + (0 if own else 1), 2)
     here = pl.ds(pl.multiple_of(half * rows, rows), rows)
     for shift, m_ref in enumerate(m_refs):
-        block = lax.rem(x_ref[0] + SIDE - shift, SIDE)
+        block = lax.rem(column + SIDE - shift, SIDE)
         for part, value in enumerate(products(m_ref[:, here, :], g_ref)):
             o_ref[block, part] = value.astype(BF16)
 
@@ -109,45 +110,38 @@
         o_ref[part] = value.astype(BF16)
 
 
-def local(kernel, outs, flops, *operands, scalars=0):
+def local(kernel, outs, flops, *operands):
     moved = sum(x.size * x.dtype.itemsize for x in operands)
     shapes = [jax.ShapeDtypeStruct(shape, BF16) for shape in outs]
     return pl.pallas_call(
         kernel,
         out_shape=shapes if len(shapes) > 1 else shapes[0],
-        in_specs=[SM] * scalars + [VM] * (len(operands) - scalars),
+        in_specs=[VM] * len(operands),
         out_specs=[VM] * len(shapes) if len(shapes) > 1 else VM,
         cost_estimate=cost(flops, moved + 2 * sum(x.size for x in shapes)),
         compiler_params=pltpu.CompilerParams(vmem_limit_bytes=LIMIT),
     )(*operands)
 
 
-def shifted_columns(here, matrix):
+def shifted_columns(matrix):
     rows, inner = matrix.shape[1:]
-    step = rows // STEPS
-    piece = (2, step, inner // SIDE)
     return pl.pallas_call(
         shift_kernel,
         out_shape=[jax.ShapeDtypeStruct((2, rows, inner // SIDE), BF16)] * SIDE,
-        grid_spec=pltpu.PrefetchScalarGridSpec(
-            num_scalar_prefetch=1,
-            grid=(STEPS,),
-            in_specs=[pl.BlockSpec((2, step, inner), lambda i, x: (0, i, 0))],
-            out_specs=[pl.BlockSpec(piece, lambda i, x: (0, i, 0))] * SIDE,
-        ),
+        in_specs=[VM],
+        out_specs=[VM] * SIDE,
         cost_estimate=cost(0, 8 * rows * inner),
-    )(here, matrix)
+    )(matrix)
 
 
 def column_blocks(matrix):
     rows, inner = matrix.shape[1:]
-    step = rows // STEPS
     return pl.pallas_call(
         split_kernel,
         out_shape=jax.ShapeDtypeStruct((SIDE, 2, rows, inner // SIDE), BF16),
-        grid=(STEPS,),
-        in_specs=[pl.BlockSpec((2, step, inner), lambda i: (0, i, 0))],
-        out_specs=pl.BlockSpec((SIDE, 2, step, inner // SIDE), lambda i: (0, 0, i, 0)),
+        grid=(2,),
+        in_specs=[pl.BlockSpec((1, rows, inner), lambda i: (i, 0, 0))],
+        out_specs=pl.BlockSpec((SIDE, 1, rows, inner // SIDE), lambda i: (0, i, 0, 0)),
         cost_estimate=cost(0, 8 * rows * inner),
     )(matrix)
 
@@ -192,7 +186,6 @@
     child_inverse, border_block, child_rhs, parent_inverse, parent_rhs, parent_of, owner, row_map
 ):
     slot_index = lax.axis_index("blk")
-    group_index = lax.axis_index("grp")
     rows, cols = child_rhs.shape[2:]
     block = (2, rows, cols)
     fan = (SIDE,) + block
@@ -200,13 +193,12 @@
     local_map = lax.dynamic_slice_in_dim(row_map, slot_index * rows, rows, 1)
     half_order = SIDE * SIDE * rows
     rows_of = (local_map // half_order) * rows + local_map % rows
-    here = jnp.stack([slot_index // SIDE, group_index % 2]).astype(jnp.int32)
 
     inverse = along_x(column_blocks(child_inverse[0]))
     source = along_y(child_rhs[0])
     parts = local(child_kernel, [fan], flops, inverse, source)
     parts = along_x(parts)
-    parent = shifted_columns(here, parent_inverse[0])
+    parent = shifted_columns(parent_inverse[0])
     parts, *parent = lax.optimization_barrier((parts, *parent))
     solved, sent = local(total_kernel, [block] * 2, 0, parts)
     source = along_y(sent)
@@ -224,7 +216,7 @@
     right = local(right_kernel, [block], 0, sums, parent_rhs[0])
     source = along_y(right)
     given, kept = (
-        local(functools.partial(parent_kernel, own), [fan], flops, here, *parent, source, scalars=1)
+        local(functools.partial(parent_kernel, own), [fan], flops, *parent, source)
         for own in (False, True)
     )
     taken = lax.ppermute(given, "grp", [(i, i ^ 1) for i in range(GROUPS)])

time: 152 us -> 152 us (level)
  Pallas kernels: 16.7 us -> 14.6 us
  waiting for transfers between devices: 0.56 us -> 2.56 us
  transfers between devices with their start and end apart: 8 -> 8, of which waited for: 2 -> 2; matrix products, arithmetic and copies ran while one was open for 1% -> 0% of each run, Pallas kernels for 6% -> 5%
where the time goes in v3:
time: 152 us; the launch traced here: 150 us
  blocking collectives  84.4 us (56%)
  starting transfers between devices  47.2 us (31%)
  Pallas kernels  14.6 us (10%)
  waiting for transfers between devices  2.56 us (2%)
    all_gather x3, blocking collectives, along_y(): lax.all_gather(block, 'blk', axis=0, tiled=False, axis_index_groups=ALONG_Y)  43.5 us
    all_to_all x3, blocking collectives, over(): lax.all_to_all(blocks, axis, 0, 0, axis_index_groups=groups, tiled=True)  41 us
    all_to_all x4, starting transfers between devices, over(): lax.all_to_all(blocks, axis, 0, 0, axis_index_groups=groups, tiled=True)  33.3 us
    ppermute x3, starting transfers between devices, shifted(): return lax.ppermute(block, 'blk', pairs)  8.41 us
    pallas_call x9, Pallas kernels, local(): pl.pallas_call(kernel, out_shape=shapes if len(shapes) > 1 else shapes[0]...  6.1 us
    ppermute x1, starting transfers between devices, per_device(): taken = lax.ppermute(given, 'grp', [(i, i ^ 1) for i in range(GROUPS)])  5.45 us
    pallas_call x2, Pallas kernels, column_blocks(): pl.pallas_call(split_kernel, out_shape=jax.ShapeDtypeStruct((SIDE, 2, row...  4.22 us
    pallas_call x1, Pallas kernels, shifted_columns(): pl.pallas_call(shift_kernel, out_shape=[jax.ShapeDtypeStruct((2, rows, in...  3.1 us
  transfers between devices with their start and end apart: 8, of which 2 were waited for; matrix products, arithmetic and copies ran while one was open for 0% of the time, Pallas kernels for 5%

profile of v3, /device:TPU:1, one launch (start us, length us, event | category | flops | bytes accessed | tf_op | source)
XLA Modules:
  0.0 150.4 jit_solution(16571940377011095224)
XLA Ops:
  0.6 2.1 %shard_map.96 = bf16[4,2,128,512]{3,2,1,0:T(8,128)(2,1)} custom-call(bf16[2,128,2048]{2,1,0:T(8,128)(2,1)} %bitcast.15), custom_call_target="tpu_custom_call" | custom-call | bytes 2097152 | tf_op jit(solution)/shard_map/pallas_call | solution.py:139
  2.8 4.8 %all-to-all-start = ((bf16[4,2,128,512]{3,2,1,0:T(8,128)(2,1)}), bf16[4,2,128,512]{3,2,1,0:T(8,128)(2,1)S(1)}, u32[]{:S(2)}, u32[]{:S(2)}) async-start(bf16[4,2,128,512]{3,2,1,0:T(8,128)(2,1)} %shard_map.96), calls=%async_computation | async-start | bytes 2097152 | tf_op jit(solution)/shard_map/all_to_all | solution.py:167
  7.6 16.0 %all_gather.15.g_ref = bf16[4,2,128,256]{3,2,1,0:T(8,128)(2,1)S(1)} all-gather(bf16[1,2,128,256]{3,2,1,0:T(8,128)(2,1)S(1)} %copy-done.4), channel_id=1, replica_groups={{0,1,2,3},{4,5,6,7},{8,9,10,11},{12,13,14,15},{16,17,18,19},{20,21,22,2..., dimensions={0}, use_global_device_ids=true | all-gather | bytes 655360 | tf_op jit(solution)/shard_map/all_gather | solution.py:178
  23.6 1.5 %shard_map.97 = bf16[4,2,128,256]{3,2,1,0:T(8,128)(2,1)} custom-call(bf16[4,2,128,512]{3,2,1,0:T(8,128)(2,1)S(1)} %all-to-all-done.m_ref, bf16[4,2,128,256]{3,2,1,0:T(8,128)(2,1)S(1)} %all_gather.15.g_ref), custom_call_target="tpu_custom_call" | custom-call | flops 536870912 | bytes 2097152 | tf_op jit(solution)/shard_map/pallas_call | solution.py:116
  25.1 4.4 %all-to-all-start.1 = ((bf16[4,2,128,256]{3,2,1,0:T(8,128)(2,1)}), bf16[4,2,128,256]{3,2,1,0:T(8,128)(2,1)S(1)}, u32[]{:S(2)}, u32[]{:S(2)}) async-start(bf16[4,2,128,256]{3,2,1,0:T(8,128)(2,1)} %shard_map.97), calls=%async_computation.1 | async-start | bytes 1048576 | tf_op jit(solution)/shard_map/all_to_all | solution.py:167
  29.5 3.1 %shard_map.98 = (bf16[2,256,512]{2,1,0:T(8,128)(2,1)}, bf16[2,256,512]{2,1,0:T(8,128)(2,1)}, bf16[2,256,512]{2,1,0:T(8,128)(2,1)}, bf16[2,256,512]{2,1,0:T(8,128)(2,1)}) custom-call(bf16[2,256,2048]{2,1,0:T(8,128)(2,1)} %bitcast.14), custom_call_target="tpu_custom_call" | custom-call | bytes 4194304 | tf_op jit(solution)/shard_map/pallas_call | solution.py:128
  32.6 2.1 %shard_map.95 = bf16[4,2,128,512]{3,2,1,0:T(8,128)(2,1)} custom-call(bf16[2,128,2048]{2,1,0:T(8,128)(2,1)} %bitcast.16), custom_call_target="tpu_custom_call" | custom-call | bytes 2097152 | tf_op jit(solution)/shard_map/pallas_call | solution.py:139
  34.7 1.8 %all-to-all-done.1.p_ref = bf16[4,2,128,256]{3,2,1,0:T(8,128)(2,1)S(1)} async-done(((bf16[4,2,128,256]{3,2,1,0:T(8,128)(2,1)}), bf16[4,2,128,256]{3,2,1,0:T(8,128)(2,1)S(1)}, u32[]{:S(2)}, u32[]{:S(2)}) %all-to-all-start.1) | async-done | bytes 524320 | tf_op jit(solution)/shard_map/all_to_all | solution.py:167
  36.5 0.7 shard_map.99
  37.2 3.5 %all-to-all-start.2 = ((bf16[4,2,128,512]{3,2,1,0:T(8,128)(2,1)}), bf16[4,2,128,512]{3,2,1,0:T(8,128)(2,1)S(1)}, u32[]{:S(2)}, u32[]{:S(2)}) async-start(bf16[4,2,128,512]{3,2,1,0:T(8,128)(2,1)} %shard_map.95), calls=%async_computation.2 | async-start | bytes 2097152 | tf_op jit(solution)/shard_map/all_to_all | solution.py:167
  40.7 13.7 %all-gather = bf16[8,128,256]{2,1,0:T(8,128)(2,1)S(1)} all-gather(bf16[2,128,256]{2,1,0:T(8,128)(2,1)S(1)} %get-tuple-element.27), channel_id=2, replica_groups={{0,1,2,3},{4,5,6,7},{8,9,10,11},{12,13,14,15},{16,17,18,19},{20,21,22,2..., dimensions={0}, use_global_device_ids=true | all-gather | bytes 655360 | tf_op jit(solution)/shard_map/all_gather | solution.py:178
  54.4 0.0 all-to-all-done.2.m_ref
  54.5 0.0 copy-start.1
  54.5 0.7 shard_map.100
  55.2 11.1 %all_to_all.35.p_ref = bf16[4,2,128,256]{3,2,1,0:T(8,128)(2,1)S(1)} all-to-all(bf16[4,2,128,256]{3,2,1,0:T(8,128)(2,1)S(1)} %shard_map.100), channel_id=1, replica_groups={{0,4,8,12},{1,5,9,13},{2,6,10,14},{3,7,11,15},{16,20,24,28},{17,21,25,2..., dimensions={0} | all-to-all | bytes 1048576 | tf_op jit(solution)/shard_map/all_to_all | solution.py:167
  66.3 0.8 shard_map.101
  67.1 20.5 %all-to-all-start.4 = ((bf16[32,16,128]{2,1,0:T(8,128)(2,1)}), bf16[32,16,128]{2,1,0:T(8,128)(2,1)S(1)}, u32[]{:S(2)}, u32[]{:S(2)}) async-start(bf16[32,16,128]{2,1,0:T(8,128)(2,1)} %shard_map.101), calls=%async_computation.4 | async-start | bytes 262144 | tf_op jit(solution)/shard_map/all_to_all | solution.py:167
  87.6 2.2 %collective-permute-start = (bf16[2,256,512]{2,1,0:T(8,128)(2,1)}, bf16[2,256,512]{2,1,0:T(8,128)(2,1)S(1)}, u32[]{:S(2)}, u32[]{:S(2)}) collective-permute-start(bf16[2,256,512]{2,1,0:T(8,128)(2,1)} %get-tuple-element.23), channel_id=1, source_target_pairs={{0,4},{1,5},{2,6},{3,7},{4,8},{5,9},{6,10},{7,11},{8,12},{9,13},{1... | collective-permute-start | bytes 1572872 | tf_op jit(solution)/shard_map/ppermute | solution.py:174
  89.8 3.7 %collective-permute-start.1 = (bf16[2,256,512]{2,1,0:T(8,128)(2,1)S(1)}, bf16[2,256,512]{2,1,0:T(8,128)(2,1)S(1)}, u32[]{:S(2)}, u32[]{:S(2)}) collective-permute-start(bf16[2,256,512]{2,1,0:T(8,128)(2,1)S(1)} %copy-done.6), channel_id=1, source_target_pairs={{0,8},{1,9},{2,10},{3,11},{4,12},{5,13},{6,14},{7,15},{8,0},{9,1},... | collective-permute-start | bytes 1572872 | tf_op jit(solution)/shard_map/ppermute | solution.py:174
  93.6 2.5 %collective-permute-start.2 = (bf16[2,256,512]{2,1,0:T(8,128)(2,1)S(1)}, bf16[2,256,512]{2,1,0:T(8,128)(2,1)S(1)}, u32[]{:S(2)}, u32[]{:S(2)}) collective-permute-start(bf16[2,256,512]{2,1,0:T(8,128)(2,1)S(1)} %copy-done.5), channel_id=1, source_target_pairs={{0,12},{1,13},{2,14},{3,15},{4,0},{5,1},{6,2},{7,3},{8,4},{9,5},{1... | collective-permute-start | bytes 1572872 | tf_op jit(solution)/shard_map/ppermute | solution.py:174
  96.1 0.7 fusion.2.rows_ref
  96.9 1.2 shard_map.102
  98.1 17.7 %all_to_all.36.b_ref = bf16[32,16,128]{2,1,0:T(8,128)(2,1)S(1)} all-to-all(bf16[32,16,128]{2,1,0:T(8,128)(2,1)S(1)} %shard_map.102), channel_id=1, replica_groups=mesh['grp'=32,'blk'=16] {'grp'}, dimensions={0} | all-to-all | bytes 262144 | tf_op jit(solution)/shard_map/all_to_all | solution.py:167
  115.8 0.1 shard_map.103
  116.0 13.8 %all-gather.1 = bf16[8,128,256]{2,1,0:T(8,128)(2,1)S(1)} all-gather(bf16[2,128,256]{2,1,0:T(8,128)(2,1)S(1)} %shard_map.103), channel_id=3, replica_groups={{0,1,2,3},{4,5,6,7},{8,9,10,11},{12,13,14,15},{16,17,18,19},{20,21,22,2..., dimensions={0}, use_global_device_ids=true | all-gather | bytes 655360 | tf_op jit(solution)/shard_map/all_gather | solution.py:178
  129.7 0.7 shard_map.105
  130.5 5.5 %collective-permute-start.3 = (bf16[4,2,128,256]{3,2,1,0:T(8,128)(2,1)S(1)}, bf16[4,2,128,256]{3,2,1,0:T(8,128)(2,1)S(1)}, u32[]{:S(2)}, u32[]{:S(2)}) collective-permute-start(bf16[4,2,128,256]{3,2,1,0:T(8,128)(2,1)S(1)} %shard_map.105), channel_id=1, source_target_pairs={{0,16},{16,0},{32,48},{48,32},{64,80},{80,64},{96,112},{112,96},{1... | collective-permute-start | bytes 1572872 | tf_op jit(solution)/shard_map/ppermute | solution.py:222
  135.9 0.7 shard_map.104.a_ref
  136.6 0.8 collective-permute-done.3.b_ref
  137.4 0.1 shard_map.106
  137.6 12.1 %all_to_all.37.p_ref = bf16[4,2,128,256]{3,2,1,0:T(8,128)(2,1)S(1)} all-to-all(bf16[4,2,128,256]{3,2,1,0:T(8,128)(2,1)S(1)} %shard_map.106), channel_id=1, replica_groups={{0,4,8,12},{1,5,9,13},{2,6,10,14},{3,7,11,15},{16,20,24,28},{17,21,25,2..., dimensions={0} | all-to-all | bytes 1048576 | tf_op jit(solution)/shard_map/all_to_all | solution.py:167
  149.7 0.7 shard_map.107
  (18 shorter events, 0.0 us)
Async XLA Ops:
  0.6 7.0 %copy-start.4 = (bf16[1,2,128,256]{3,2,1,0:T(8,128)(2,1)S(1)}, bf16[1,2,128,256]{3,2,1,0:T(8,128)(2,1)}, u32[]{:S(2)}) copy-start(bf16[1,2,128,256]{3,2,1,0:T(8,128)(2,1)} %param.10) | copy-start | bytes 393220
  2.8 20.8 %all-to-all-start = ((bf16[4,2,128,512]{3,2,1,0:T(8,128)(2,1)}), bf16[4,2,128,512]{3,2,1,0:T(8,128)(2,1)S(1)}, u32[]{:S(2)}, u32[]{:S(2)}) async-start(bf16[4,2,128,512]{3,2,1,0:T(8,128)(2,1)} %shard_map.96), calls=%async_computation | async-start | bytes 2097152 | tf_op jit(solution)/shard_map/all_to_all | solution.py:167
  25.1 11.4 %all-to-all-start.1 = ((bf16[4,2,128,256]{3,2,1,0:T(8,128)(2,1)}), bf16[4,2,128,256]{3,2,1,0:T(8,128)(2,1)S(1)}, u32[]{:S(2)}, u32[]{:S(2)}) async-start(bf16[4,2,128,256]{3,2,1,0:T(8,128)(2,1)} %shard_map.97), calls=%async_computation.1 | async-start | bytes 1048576 | tf_op jit(solution)/shard_map/all_to_all | solution.py:167
  37.2 17.3 %all-to-all-start.2 = ((bf16[4,2,128,512]{3,2,1,0:T(8,128)(2,1)}), bf16[4,2,128,512]{3,2,1,0:T(8,128)(2,1)S(1)}, u32[]{:S(2)}, u32[]{:S(2)}) async-start(bf16[4,2,128,512]{3,2,1,0:T(8,128)(2,1)} %shard_map.95), calls=%async_computation.2 | async-start | bytes 2097152 | tf_op jit(solution)/shard_map/all_to_all | solution.py:167
  54.4 35.4 %copy-start.6 = (bf16[2,256,512]{2,1,0:T(8,128)(2,1)S(1)}, bf16[2,256,512]{2,1,0:T(8,128)(2,1)}, u32[]{:S(2)}) copy-start(bf16[2,256,512]{2,1,0:T(8,128)(2,1)} %get-tuple-element.24) | copy-start | bytes 1572868
  54.4 39.1 %copy-start.5 = (bf16[2,256,512]{2,1,0:T(8,128)(2,1)S(1)}, bf16[2,256,512]{2,1,0:T(8,128)(2,1)}, u32[]{:S(2)}) copy-start(bf16[2,256,512]{2,1,0:T(8,128)(2,1)} %get-tuple-element.25) | copy-start | bytes 1572868
  54.4 42.4 %copy-start.2 = (s32[32,1]{0,1:T(1,128)S(1)}, s32[32,1]{0,1:T(1,128)}, u32[]{:S(2)}) copy-start(s32[32,1]{0,1:T(1,128)} %param.13) | copy-start | bytes 388
  54.4 42.4 %copy-start.3 = (s32[16]{0:T(128)S(1)}, s32[16]{0:T(128)}, u32[]{:S(2)}) copy-start(s32[16]{0:T(128)} %owner_ref.1) | copy-start | bytes 196
  54.5 61.4 %copy-start.1 = (bf16[1,2,128,256]{3,2,1,0:T(8,128)(2,1)S(1)}, bf16[1,2,128,256]{3,2,1,0:T(8,128)(2,1)}, u32[]{:S(2)}) copy-start(bf16[1,2,128,256]{3,2,1,0:T(8,128)(2,1)} %param.12) | copy-start | bytes 393220
  55.2 74.5 %copy-start = (bf16[2,256,512]{2,1,0:T(8,128)(2,1)S(1)}, bf16[2,256,512]{2,1,0:T(8,128)(2,1)}, u32[]{:S(2)}) copy-start(bf16[2,256,512]{2,1,0:T(8,128)(2,1)} %get-tuple-element.22.refs_0_) | copy-start | bytes 1572868
  67.1 29.8 %all-to-all-start.4 = ((bf16[32,16,128]{2,1,0:T(8,128)(2,1)}), bf16[32,16,128]{2,1,0:T(8,128)(2,1)S(1)}, u32[]{:S(2)}, u32[]{:S(2)}) async-start(bf16[32,16,128]{2,1,0:T(8,128)(2,1)} %shard_map.101), calls=%async_computation.4 | async-start | bytes 262144 | tf_op jit(solution)/shard_map/all_to_all | solution.py:167
  87.6 42.1 %collective-permute-start = (bf16[2,256,512]{2,1,0:T(8,128)(2,1)}, bf16[2,256,512]{2,1,0:T(8,128)(2,1)S(1)}, u32[]{:S(2)}, u32[]{:S(2)}) collective-permute-start(bf16[2,256,512]{2,1,0:T(8,128)(2,1)} %get-tuple-element.23), channel_id=1, source_target_pairs={{0,4},{1,5},{2,6},{3,7},{4,8},{5,9},{6,10},{7,11},{8,12},{9,13},{1... | collective-permute-start | bytes 1572872 | tf_op jit(solution)/shard_map/ppermute | solution.py:174
  89.8 39.9 %collective-permute-start.1 = (bf16[2,256,512]{2,1,0:T(8,128)(2,1)S(1)}, bf16[2,256,512]{2,1,0:T(8,128)(2,1)S(1)}, u32[]{:S(2)}, u32[]{:S(2)}) collective-permute-start(bf16[2,256,512]{2,1,0:T(8,128)(2,1)S(1)} %copy-done.6), channel_id=1, source_target_pairs={{0,8},{1,9},{2,10},{3,11},{4,12},{5,13},{6,14},{7,15},{8,0},{9,1},... | collective-permute-start | bytes 1572872 | tf_op jit(solution)/shard_map/ppermute | solution.py:174
  93.6 36.2 %collective-permute-start.2 = (bf16[2,256,512]{2,1,0:T(8,128)(2,1)S(1)}, bf16[2,256,512]{2,1,0:T(8,128)(2,1)S(1)}, u32[]{:S(2)}, u32[]{:S(2)}) collective-permute-start(bf16[2,256,512]{2,1,0:T(8,128)(2,1)S(1)} %copy-done.5), channel_id=1, source_target_pairs={{0,12},{1,13},{2,14},{3,15},{4,0},{5,1},{6,2},{7,3},{8,4},{9,5},{1... | collective-permute-start | bytes 1572872 | tf_op jit(solution)/shard_map/ppermute | solution.py:174
  130.5 7.0 %collective-permute-start.3 = (bf16[4,2,128,256]{3,2,1,0:T(8,128)(2,1)S(1)}, bf16[4,2,128,256]{3,2,1,0:T(8,128)(2,1)S(1)}, u32[]{:S(2)}, u32[]{:S(2)}) collective-permute-start(bf16[4,2,128,256]{3,2,1,0:T(8,128)(2,1)S(1)} %shard_map.105), channel_id=1, source_target_pairs={{0,16},{16,0},{32,48},{48,32},{64,80},{80,64},{96,112},{112,96},{1... | collective-permute-start | bytes 1572872 | tf_op jit(solution)/shard_map/ppermute | solution.py:222
